TPU v7x, 128 devices: a whole 4x4x4 slice. The times are simulated.
128 devices in a mesh: seq: 4 (over z_lo, core), blk: 32 (over y, x, z_hi).
Axes of the slice: x: 4, y: 4, z: 4 (z_hi: 2, z_lo: 2; z = z_hi * 2 + z_lo), core: 2. Of those that a mesh axis runs over, the one named last changes fastest.
Arguments:
- patches: bfloat16 [32768, 1280], P(('seq', 'blk')), may hold values from -40 to 40
- vis_gain: float32 [1280], replicated, may hold values from 0.1 to 1.9
- vis_up: bfloat16 [5120, 1280], P('seq'), may hold values from -0.15625 to 0.15625
- vis_bias: float32 [5120], P('seq'), may hold values from -4 to 4
- vis_down: bfloat16 [5120, 1280], P('seq'), may hold values from -0.078125 to 0.078125
- merge_gain: float32 [1280], replicated, may hold values from 0.1 to 1.9
- merge_proj: bfloat16 [5120, 1280], replicated, may hold values from -0.078125 to 0.078125
- text_embed: bfloat16 [16384, 1280], P(('seq', 'blk')), may hold values from -40 to 40
- slot_index: int32 [8192], P(('seq', 'blk')), may hold values from 0 to 16383, as said below
- text_gain: float32 [1280], replicated, may hold values from 0.1 to 1.9
- text_up: bfloat16 [5120, 1280], P('blk'), may hold values from -0.15625 to 0.15625
- text_down: bfloat16 [5120, 1280], P('blk'), may hold values from -0.078125 to 0.078125
Outputs:
- hidden_out: bfloat16 [16384, 1280], P(('seq', 'blk'))
Inputs may be any that keep to these rules, and one draw needn't show every extreme that they name: slot_index values are distinct. The merged rows held by one device go to prompt tokens held by devices with the same seq index. Each device sends either no merged rows or exactly 4 merged rows to each device of its blk group; in every draw some device receives 4 rows from every device of its blk group.
All inputs are finite; a program needn't handle non-finite values.
Results may differ from a plain program's by a relative error of at most 0.015.
Values may be sent and summed in bfloat16 or wider, within the bound.
A program may use at most 192 MiB of HBM per device.

v0:
```python
import jax
import jax.numpy as jnp
from jax import lax
from jax.sharding import PartitionSpec as P


def normalize(values, row_gain):
    values = values.astype(jnp.float32)
    center = values - jnp.mean(values, axis=-1, keepdims=True)
    spread = jnp.mean(center * center, axis=-1, keepdims=True)
    return center * lax.rsqrt(spread + 1e-06) * row_gain


def up_project(rows_in, up_piece):
    return lax.dot_general(
        rows_in, up_piece, (((1,), (1,)), ((), ())), preferred_element_type=jnp.float32
    )


def per_device(
    patches,
    vis_gain,
    vis_up,
    vis_bias,
    vis_down,
    merge_gain,
    merge_proj,
    text_embed,
    slot_index,
    text_gain,
    text_up,
    text_down,
):
    rows_here = patches.shape[0]
    width = patches.shape[1]
    vis_normed = normalize(patches, vis_gain).astype(jnp.bfloat16)
    gathered = lax.all_gather(vis_normed, "seq", axis=0, tiled=True)
    sliced = gathered
    hidden = jax.nn.gelu(up_project(sliced, vis_up) + vis_bias, approximate=True).astype(
        jnp.bfloat16
    )
    vis_mlp = lax.psum_scatter(
        jnp.dot(hidden, vis_down, preferred_element_type=jnp.float32).astype(jnp.bfloat16),
        "seq",
        scatter_dimension=0,
        tiled=True,
    ).astype(jnp.float32)
    vis_out = patches.astype(jnp.float32) + vis_mlp
    merge_normed = normalize(vis_out, merge_gain).astype(jnp.bfloat16)
    joined = merge_normed.reshape(rows_here // 4, 4 * width)
    merged = jnp.dot(joined, merge_proj, preferred_element_type=jnp.float32).astype(jnp.bfloat16)
    cycle_size = lax.axis_size("blk")
    merged_count = slot_index.shape[0]
    token_count = text_embed.shape[0]
    capacity = 2 * merged_count // cycle_size
    target = slot_index // token_count % cycle_size
    position = slot_index % token_count
    one_hot = (target[:, None] == jnp.arange(cycle_size, dtype=jnp.int32)[None, :]).astype(
        jnp.int32
    )
    rank_in = jnp.sum((jnp.cumsum(one_hot, axis=0) - one_hot) * one_hot, axis=1)
    buffer_slot = target * capacity + rank_in
    send_rows = jnp.zeros((cycle_size * capacity, width), jnp.bfloat16).at[buffer_slot].set(merged)
    send_where = (
        jnp.full((cycle_size * capacity,), token_count, jnp.int32).at[buffer_slot].set(position)
    )
    got_rows, got_where = (
        lax.all_to_all(send_rows, "blk", split_axis=0, concat_axis=0, tiled=True),
        lax.all_to_all(send_where, "blk", split_axis=0, concat_axis=0, tiled=True),
    )
    text_rows = text_embed.at[got_where].set(got_rows, mode="drop")
    text_normed = normalize(text_rows, text_gain).astype(jnp.bfloat16)
    gathered_tokens = lax.all_gather(text_normed, "blk", axis=0, tiled=True)
    sliced = gathered_tokens
    hidden = jax.nn.gelu(up_project(sliced, text_up), approximate=True).astype(jnp.bfloat16)
    text_mlp = lax.psum_scatter(
        jnp.dot(hidden, text_down, preferred_element_type=jnp.float32).astype(jnp.bfloat16),
        "blk",
        scatter_dimension=0,
        tiled=True,
    ).astype(jnp.float32)
    return (text_rows.astype(jnp.float32) + text_mlp).astype(jnp.bfloat16)


def solution(mesh):
    placed = (
        P(("seq", "blk"), None),
        P(),
        P("seq", None),
        P("seq"),
        P("seq", None),
        P(),
        P(),
        P(("seq", "blk"), None),
        P(("seq", "blk")),
        P(),
        P("blk", None),
        P("blk", None),
    )
    return jax.shard_map(
        per_device, mesh=mesh, in_specs=placed, out_specs=P(("seq", "blk"), None), check_vma=False
    )
```

profile of v0, /device:TPU:1, one launch (start us, length us, event | category | flops | bytes accessed | tf_op | source)
XLA Modules:
  0.0 506.6 jit_solution(16721115302343496381)
XLA Ops:
  6.5 0.0 copy-start
  6.5 0.0 copy-start.5
  6.5 0.0 all-gather.3.cloned.1.call-start
  6.5 1.9 copy.16
  8.4 1.3 convert_reduce_fusion
  9.7 1.4 fusion.18
  11.1 2.2 fusion.20
  13.3 0.0 all-gather.3.cloned.1.call-update
  13.3 0.0 reduce-scatter.3.cloned.1.call-start
  13.4 37.3 %all-gather.3.cloned.1.call-done = bf16[1024,1280]{1,0:T(8,128)(2,1)} async-done(((bf16[256,1280]{1,0:T(8,128)(2,1)}), bf16[1024,1280]{1,0:T(8,128)(2,1)}) %all-gather.3.cloned.1.call-update) | async-done | bytes 2621456 | tf_op jit(solution)/shard_map/all_gather | solution.py:37
  50.6 0.0 copy-done
  50.6 0.0 copy-done.5
  50.6 11.0 %convolution_convert_fusion.1 = bf16[1024,1280]{1,0:T(8,128)(2,1)} fusion(bf16[1280,1280]{1,0:T(8,128)(2,1)S(1)} %copy-done, bf16[1024,1280]{1,0:T(8,128)(2,1)} %all-gather.3.cloned.1.call-done, bf16[1280,1280]{1,0:T(8,128)(2,1)} %param.14, f32[1280]{0:T(1024)S(1)} %copy-done.5), kind=kOutput, calls=%fused_computation.14 | convolution fusion | flops 6725304320 | bytes 11801600 | tf_op jit(solution)/shard_map/dot_general | solution.py:43
  61.7 0.0 copy-start.6
  61.7 0.0 copy-start.3
  61.7 0.0 reduce-scatter.3.cloned.1.call-update
  61.7 0.6 copy-done.6
  62.3 0.1 fusion.36
  62.4 0.1 reduce_window_sum.11
  62.5 0.2 select_reduce_fusion
  62.7 0.8 scatter_custom_fusion
  63.5 0.7 all_to_all.16
  64.2 9.1 %all-to-all-start = ((s32[32,4,1]{1,2,0:T(1,128)}), s32[32,4,1]{1,2,0:T(1,128)S(1)}, u32[]{:S(2)}, u32[]{:S(2)}) async-start(s32[32,4,1]{1,2,0:T(1,128)} %bitcast), calls=%async_computation | async-start | bytes 32768 | tf_op jit(solution)/shard_map/all_to_all | solution.py:69
  73.3 22.0 %reduce-scatter.3.cloned.1.call-done = bf16[256,1280]{1,0:T(8,128)(2,1)} async-done(((bf16[1024,1280]{1,0:T(8,128)(2,1)}), bf16[256,1280]{1,0:T(8,128)(2,1)}) %reduce-scatter.3.cloned.1.call-update) | async-done | bytes 655376 | tf_op jit(solution)/shard_map/reduce_scatter | solution.py:42
  95.3 0.0 copy-start.1
  95.3 0.0 copy-start.2
  95.3 1.6 fusion.27
  96.9 1.6 multiply_reduce_fusion
  98.6 0.0 copy-done.3
  98.6 0.0 copy-done.1
  98.6 0.0 copy-done.2
  98.6 1.1 multiply_convert_fusion
  99.8 2.3 reshape.76
  102.0 7.3 %convolution_convert_fusion.2 = bf16[64,1280]{1,0:T(8,128)(2,1)S(1)} fusion(bf16[64,5120]{1,0:T(8,128)(2,1)} %reshape.76, bf16[5120,1280]{1,0:T(8,128)(2,1)} %param.18), kind=kOutput, calls=%fused_computation.23 | convolution fusion | flops 838942720 | bytes 13926400 | tf_op jit(solution)/shard_map/dot_general | solution.py:51
  109.3 1.6 scatter_custom_fusion.1
  110.9 1.8 all_to_all.19
  112.7 0.0 all-to-all-done
  112.7 9.2 %all-to-all-start.1 = ((bf16[32,4,1280]{2,1,0:T(4,128)(2,1)}), bf16[32,4,1280]{2,1,0:T(4,128)(2,1)}, u32[]{:S(2)}, u32[]{:S(2)}) async-start(bf16[32,4,1280]{2,1,0:T(4,128)(2,1)} %all_to_all.19), calls=%async_computation.2 | async-start | bytes 655360 | tf_op jit(solution)/shard_map/all_to_all | solution.py:68
  121.9 0.0 all-gather.5.cloned.1.call-start
  122.0 0.5 broadcast.138
  122.5 0.7 reduce.3
  123.2 0.1 all_to_all.18
  123.3 9.4 %all-to-all-done.1 = bf16[32,4,1280]{2,1,0:T(4,128)(2,1)} async-done(((bf16[32,4,1280]{2,1,0:T(4,128)(2,1)}), bf16[32,4,1280]{2,1,0:T(4,128)(2,1)}, u32[]{:S(2)}, u32[]{:S(2)}) %all-to-all-start.1) | async-done | bytes 327712 | tf_op jit(solution)/shard_map/all_to_all | solution.py:68
  132.6 1.8 reshape.97
  134.4 0.0 copy-start.4
  134.4 3.3 scatter_fusion
  137.7 1.1 convert_reduce_fusion.1
  138.8 1.2 fusion.30
  140.0 0.0 copy-done.4
  140.0 1.9 fusion.32
  141.9 0.0 all-gather.5.cloned.1.call-update
  142.0 0.2 reduce-scatter.5.cloned.1.call-start
  142.2 113.2 %all-gather.5.cloned.1.call-done = bf16[4096,1280]{1,0:T(8,128)(2,1)} async-done(((bf16[128,1280]{1,0:T(8,128)(2,1)}), bf16[4096,1280]{1,0:T(8,128)(2,1)}) %all-gather.5.cloned.1.call-update) | async-done | bytes 10485776 | tf_op jit(solution)/shard_map/all_gather | solution.py:73
  255.4 11.6 %convolution_convert_fusion = bf16[4096,1280]{1,0:T(8,128)(2,1)} fusion(bf16[160,1280]{1,0:T(8,128)(2,1)} %param.23, bf16[4096,1280]{1,0:T(8,128)(2,1)} %all-gather.5.cloned.1.call-done, bf16[160,1280]{1,0:T(8,128)(2,1)} %param.22), kind=kOutput, calls=%fused_computation.3 | convolution fusion | flops 3366584320 | bytes 21790720 | tf_op jit(solution)/shard_map/dot_general | solution.py:77
  267.0 0.0 reduce-scatter.5.cloned.1.call-update
  267.0 231.2 %reduce-scatter.5.cloned.1.call-done = bf16[128,1280]{1,0:T(8,128)(2,1)} async-done(((bf16[4096,1280]{1,0:T(8,128)(2,1)}), bf16[128,1280]{1,0:T(8,128)(2,1)}) %reduce-scatter.5.cloned.1.call-update) | async-done | bytes 327696 | tf_op jit(solution)/shard_map/reduce_scatter | solution.py:76
  498.2 1.9 fusion.33
  (9 shorter events, 0.1 us)
Async XLA Ops:
  6.5 44.1 %copy-start = (bf16[1280,1280]{1,0:T(8,128)(2,1)S(1)}, bf16[1280,1280]{1,0:T(8,128)(2,1)}, u32[]{:S(2)}) copy-start(bf16[1280,1280]{1,0:T(8,128)(2,1)} %param.16) | copy-start | bytes 9830404
  6.5 44.1 %copy-start.5 = (f32[1280]{0:T(1024)S(1)}, f32[1280]{0:T(1024)}, u32[]{:S(2)}) copy-start(f32[1280]{0:T(1024)} %param.15) | copy-start | bytes 15364
  6.5 44.1 %all-gather.3.cloned.1.call-start = ((), (), s32[]{:S(2)}) async-start(), calls=%async_computation.4 | async-start | bytes 3276800 | tf_op jit(solution)/shard_map/all_gather | solution.py:37
  13.3 82.0 %reduce-scatter.3.cloned.1.call-start = ((), (), s32[]{:S(2)}) async-start(), calls=%async_computation.5 | async-start | bytes 3276800 | tf_op jit(solution)/shard_map/reduce_scatter | solution.py:42
  61.7 0.7 copy-start.6
  61.7 36.9 %copy-start.3 = (f32[1280]{0:T(1024)S(1)}, f32[1280]{0:T(1024)}, u32[]{:S(2)}) copy-start(f32[1280]{0:T(1024)} %param.17) | copy-start | bytes 15364
  64.2 48.5 %all-to-all-start = ((s32[32,4,1]{1,2,0:T(1,128)}), s32[32,4,1]{1,2,0:T(1,128)S(1)}, u32[]{:S(2)}, u32[]{:S(2)}) async-start(s32[32,4,1]{1,2,0:T(1,128)} %bitcast), calls=%async_computation | async-start | bytes 32768 | tf_op jit(solution)/shard_map/all_to_all | solution.py:69
  95.3 3.3 copy-start.1
  95.3 3.3 copy-start.2
  112.7 19.9 %all-to-all-start.1 = ((bf16[32,4,1280]{2,1,0:T(4,128)(2,1)}), bf16[32,4,1280]{2,1,0:T(4,128)(2,1)}, u32[]{:S(2)}, u32[]{:S(2)}) async-start(bf16[32,4,1280]{2,1,0:T(4,128)(2,1)} %all_to_all.19), calls=%async_computation.2 | async-start | bytes 655360 | tf_op jit(solution)/shard_map/all_to_all | solution.py:68
  121.9 133.5 %all-gather.5.cloned.1.call-start = ((), (), s32[]{:S(2)}) async-start(), calls=%async_computation.6 | async-start | bytes 10813440 | tf_op jit(solution)/shard_map/all_gather | solution.py:73
  134.4 5.6 %copy-start.4 = (f32[1280]{0:T(1024)S(1)}, f32[1280]{0:T(1024)}, u32[]{:S(2)}) copy-start(f32[1280]{0:T(1024)} %param.21) | copy-start | bytes 15364
  142.0 356.3 %reduce-scatter.5.cloned.1.call-start = ((), (), s32[]{:S(2)}) async-start(), calls=%async_computation.7 | async-start | bytes 10813440 | tf_op jit(solution)/shard_map/reduce_scatter | solution.py:76
Sparse Core Ops, SparseCore 0:
  13.4 37.1 all-gather.2
  61.8 33.4 reduce-scatter.2
  142.1 113.2 all-gather.4
  267.1 231.0 reduce-scatter.4
where the time goes:
time: 509 us; the launch traced here: 507 us
  waiting for transfers between devices  413 us (81%)
  matrix products  29.9 us (6%)
  starting transfers between devices  18.6 us (4%)
  other arithmetic  16.5 us (3%)
  local copies, waits for them, and re-layouts  15.3 us (3%)
  between operations  13.2 us (3%)
    reduce_scatter x1, waiting for transfers between devices, per_device(): lax.psum_scatter(jnp.dot(hidden, text_down, preferred_element_type=jnp.fl...  231 us
    all_gather x1, waiting for transfers between devices, per_device(): gathered_tokens = lax.all_gather(text_normed, 'blk', axis=0, tiled=True)  113 us
    all_gather x1, waiting for transfers between devices, per_device(): gathered = lax.all_gather(vis_normed, 'seq', axis=0, tiled=True)  37.3 us
    reduce_scatter x1, waiting for transfers between devices, per_device(): lax.psum_scatter(jnp.dot(hidden, vis_down, preferred_element_type=jnp.flo...  22 us
    dot_general x1, matrix products, per_device(): jnp.dot(hidden, text_down, preferred_element_type=jnp.float32)  11.6 us
    dot_general x1, matrix products, per_device(): jnp.dot(hidden, vis_down, preferred_element_type=jnp.float32)  11 us
  transfers between devices with their start and end apart: 6, of which 5 were waited for; matrix products, arithmetic and copies ran while one was open for 4% of the time, Pallas kernels for 0%

commit v1 on v0

v1 whole, which is shorter than its diff:
```python
import jax
import jax.numpy as jnp
from jax import lax
from jax.sharding import PartitionSpec as P


def normalize(values, row_gain):
    values = values.astype(jnp.float32)
    center = values - jnp.mean(values, axis=-1, keepdims=True)
    spread = jnp.mean(center * center, axis=-1, keepdims=True)
    return center * lax.rsqrt(spread + 1e-06) * row_gain


def up_project(rows_in, up_piece):
    return lax.dot_general(
        rows_in, up_piece, (((1,), (1,)), ((), ())), preferred_element_type=jnp.float32
    )


def before(mask):
    size = mask.shape[1]
    ahead = (jnp.arange(size)[:, None] < jnp.arange(size)[None, :]).astype(jnp.bfloat16)
    return jnp.dot(
        mask.astype(jnp.bfloat16), ahead, preferred_element_type=jnp.float32
    ).astype(jnp.int32)


def per_device(
    patches,
    vis_gain,
    vis_up,
    vis_bias,
    vis_down,
    merge_gain,
    merge_proj,
    text_embed,
    slot_index,
    text_gain,
    text_up,
    text_down,
):
    rows_here, width = patches.shape
    seq_size, cycle_size = lax.axis_size("seq"), lax.axis_size("blk")
    seq, blk = lax.axis_index("seq"), lax.axis_index("blk")
    token_count = text_embed.shape[0]
    merged_count = slot_index.shape[0]
    capacity = 2 * merged_count // cycle_size

    piece = text_up.shape[0] // seq_size
    mine = jnp.concatenate(
        [
            lax.dynamic_slice_in_dim(text_up, seq * piece, piece, 0),
            lax.dynamic_slice_in_dim(text_down, seq * piece, piece, 0),
        ],
        axis=0,
    )
    weights = lax.all_gather(mine, "blk", axis=0)
    all_slots = lax.all_gather(slot_index, "blk", axis=0)

    vis_normed = normalize(patches, vis_gain).astype(jnp.bfloat16)
    gathered = lax.all_gather(vis_normed, "seq", axis=0, tiled=True)
    hidden = jax.nn.gelu(up_project(gathered, vis_up) + vis_bias, approximate=True).astype(
        jnp.bfloat16
    )
    vis_mlp = lax.psum_scatter(
        jnp.dot(hidden, vis_down, preferred_element_type=jnp.float32).astype(jnp.bfloat16),
        "seq",
        scatter_dimension=0,
        tiled=True,
    ).astype(jnp.float32)
    vis_out = patches.astype(jnp.float32) + vis_mlp
    merge_normed = normalize(vis_out, merge_gain).astype(jnp.bfloat16)
    joined = merge_normed.reshape(rows_here // 4, 4 * width)
    merged = jnp.dot(joined, merge_proj, preferred_element_type=jnp.float32).astype(jnp.bfloat16)

    target = slot_index // token_count % cycle_size
    to_target = jnp.arange(cycle_size, dtype=jnp.int32)[:, None] == target[None, :]
    rank = jnp.sum(jnp.where(to_target, before(to_target), 0), axis=0)
    slot = target * capacity + rank
    pick = (jnp.arange(cycle_size * capacity)[:, None] == slot[None, :]).astype(jnp.bfloat16)
    send_rows = jnp.dot(pick, merged, preferred_element_type=jnp.float32).astype(jnp.bfloat16)
    got_rows = lax.all_to_all(send_rows, "blk", split_axis=0, concat_axis=0, tiled=True)

    for_me = (all_slots // token_count % cycle_size) == blk
    rank_in = before(for_me)
    chosen = for_me[:, None, :] & (
        rank_in[:, None, :] == jnp.arange(capacity, dtype=jnp.int32)[None, :, None]
    )
    where = jnp.sum(jnp.where(chosen, (all_slots % token_count)[:, None, :] + 1, 0), axis=2) - 1
    place = jnp.arange(token_count, dtype=jnp.int32)[:, None] == where.reshape(1, -1)
    placed = jnp.dot(
        place.astype(jnp.bfloat16), got_rows, preferred_element_type=jnp.float32
    ).astype(jnp.bfloat16)
    text_rows = jnp.where(jnp.any(place, axis=1, keepdims=True), placed, text_embed)

    text_normed = normalize(text_rows, text_gain).astype(jnp.bfloat16)
    gathered_tokens = lax.all_gather(text_normed, "seq", axis=0, tiled=True)
    up_part = weights[:, :piece].reshape(-1, width)
    down_part = weights[:, piece:].reshape(-1, width)
    hidden = jax.nn.gelu(up_project(gathered_tokens, up_part), approximate=True).astype(
        jnp.bfloat16
    )
    text_mlp = lax.psum_scatter(
        jnp.dot(hidden, down_part, preferred_element_type=jnp.float32).astype(jnp.bfloat16),
        "seq",
        scatter_dimension=0,
        tiled=True,
    ).astype(jnp.float32)
    return (text_rows.astype(jnp.float32) + text_mlp).astype(jnp.bfloat16)


def solution(mesh):
    placed = (
        P(("seq", "blk"), None),
        P(),
        P("seq", None),
        P("seq"),
        P("seq", None),
        P(),
        P(),
        P(("seq", "blk"), None),
        P(("seq", "blk")),
        P(),
        P("blk", None),
        P("blk", None),
    )
    return jax.shard_map(
        per_device, mesh=mesh, in_specs=placed, out_specs=P(("seq", "blk"), None), check_vma=False
    )
```

time: 509 us -> 227 us (0.45)
  waiting for transfers between devices: 413 us -> 128 us
  blocking collectives: 0 us -> 16.5 us
  starting transfers between devices: 18.6 us -> 9.55 us
    reduce_scatter x1, waiting for transfers between devices: 231 us -> 22.7 us  [per_device(): lax.psum_scatter(jnp.dot(hidden, down_part, preferred_element_type=jnp.fl...]
    all_gather x1 -> x2, waiting for transfers between devices: 113 us -> 42.7 us  [the longest x1 27.7 us: per_device(): weights = lax.all_gather(mine, 'blk', axis=0)]
    unnamed x0 -> x1, blocking collectives: none -> 16.5 us
    all_to_all x1 -> x0, starting transfers between devices: 9.11 us -> none  [per_device(): lax.all_to_all(send_where, 'blk', split_axis=0, concat_axis=0, tiled=True)]
    reduce_scatter x1, waiting for transfers between devices: 22 us -> 14.7 us  [per_device(): lax.psum_scatter(jnp.dot(hidden, vis_down, preferred_element_type=jnp.flo...]
    slice x0 -> x1, local copies, waits for them, and re-layouts: none -> 6.05 us  [per_device(): up_part = weights[:, :piece].reshape(-1, width)]
    scatter x3 -> x0, local copies, waits for them, and re-layouts: 5.65 us -> none  [the longest x1 3.27 us: per_device(): text_rows = text_embed.at[got_where].set(got_rows, mode='drop')]
    dot_general x2 -> x5, matrix products: 18.9 us -> 18.1 us  [the longest x1 8.26 us: per_device(): jnp.dot(pick, merged, preferred_element_type=jnp.float32)]
  transfers between devices with their start and end apart: 6 -> 6, of which waited for: 5 -> 6; matrix products, arithmetic and copies ran while one was open for 4% -> 12% of each run, Pallas kernels for 0% -> 0%
where the time goes in v1:
time: 227 us
  waiting for transfers between devices  128 us (56%)
  matrix products  29.2 us (13%)
  blocking collectives  16.5 us (7%)
  between operations  15.4 us (7%)
  local copies, waits for them, and re-layouts  14.6 us (6%)
  other arithmetic  13.5 us (6%)
  starting transfers between devices  9.55 us (4%)
    all_gather x1, waiting for transfers between devices, per_device(): gathered = lax.all_gather(vis_normed, 'seq', axis=0, tiled=True)  37.3 us
    all_gather x1, waiting for transfers between devices, per_device(): weights = lax.all_gather(mine, 'blk', axis=0)  27.7 us
    reduce_scatter x1, waiting for transfers between devices, per_device(): lax.psum_scatter(jnp.dot(hidden, down_part, preferred_element_type=jnp.fl...  22.7 us
    unnamed x1, blocking collectives  16.5 us
    all_gather x1, waiting for transfers between devices, per_device(): gathered_tokens = lax.all_gather(text_normed, 'seq', axis=0, tiled=True)  15 us
    reduce_scatter x1, waiting for transfers between devices, per_device(): lax.psum_scatter(jnp.dot(hidden, vis_down, preferred_element_type=jnp.flo...  14.7 us
    dot_general x1, matrix products, per_device(): jnp.dot(hidden, vis_down, preferred_element_type=jnp.float32)  11.1 us
    all_to_all x1, waiting for transfers between devices, per_device(): lax.all_to_all(send_rows, 'blk', split_axis=0, concat_axis=0, tiled=True)  10.4 us
  transfers between devices with their start and end apart: 6, of which 6 were waited for; matrix products, arithmetic and copies ran while one was open for 12% of the time, Pallas kernels for 0%

profile of v1, /device:TPU:1, one launch (start us, length us, event | category | flops | bytes accessed | tf_op | source)
XLA Modules:
  0.0 226.7 jit_solution(18320549330211125357)
XLA Ops:
  7.4 0.0 copy-start
  7.4 0.0 copy-start.6
  7.4 0.0 all-gather.6.cloned.1.call-start
  7.4 1.4 convert_reduce_fusion
  8.8 1.4 fusion.20
  10.2 2.2 fusion.22
  12.4 0.0 all-gather.6.cloned.1.call-update
  12.4 0.0 reduce-scatter.3.cloned.1.call-start
  12.5 37.3 %all-gather.6.cloned.1.call-done = bf16[1024,1280]{1,0:T(8,128)(2,1)} async-done(((bf16[256,1280]{1,0:T(8,128)(2,1)}), bf16[1024,1280]{1,0:T(8,128)(2,1)}) %all-gather.6.cloned.1.call-update) | async-done | bytes 2621456 | tf_op jit(solution)/shard_map/all_gather | solution.py:61
  49.8 0.0 copy-done
  49.8 0.0 copy-done.6
  49.8 11.1 %convolution_convert_fusion = bf16[1024,1280]{1,0:T(8,128)(2,1)} fusion(bf16[1280,1280]{1,0:T(8,128)(2,1)S(1)} %copy-done, bf16[1024,1280]{1,0:T(8,128)(2,1)} %all-gather.6.cloned.1.call-done, bf16[1280,1280]{1,0:T(8,128)(2,1)} %param.14, f32[1280]{0:T(1024)S(1)} %copy-done.6), kind=kOutput, calls=%fused_computation.10 | convolution fusion | flops 6725304320 | bytes 11801600 | tf_op jit(solution)/shard_map/dot_general | solution.py:66
  60.9 0.0 copy-start.8
  60.9 0.0 copy-start.7
  60.9 0.0 copy-start.4
  60.9 0.0 reduce-scatter.3.cloned.1.call-update
  60.9 0.0 all-gather.10.cloned.1.call-start
  61.0 1.0 constant_dynamic-slice_fusion
  61.9 0.7 pad_maximum_fusion
  62.6 0.0 all-gather.10.cloned.1.call-update
  62.6 0.0 copy-done.8
  62.6 0.6 dynamic-slice
  63.9 0.0 copy-done.7
  63.9 0.3 dynamic-update-slice
  64.2 16.5 %all-reduce = s32[2048]{0:T(1024)S(1)} all-reduce(s32[2048]{0:T(1024)S(1)} %dynamic-update-slice), channel_id=2, replica_groups=mesh['seq'=4,'blk'=32] {'blk'}, use_global_device_ids=true, to_apply=%add | all-reduce | flops 2048 | bytes 16384
  80.7 0.1 reshape.69
  80.8 0.1 fusion.31
  81.0 0.1 convolution_convert_fusion.6
  81.1 0.1 select_reduce_fusion
  81.3 14.7 %reduce-scatter.3.cloned.1.call-done = bf16[256,1280]{1,0:T(8,128)(2,1)} async-done(((bf16[1024,1280]{1,0:T(8,128)(2,1)}), bf16[256,1280]{1,0:T(8,128)(2,1)}) %reduce-scatter.3.cloned.1.call-update) | async-done | bytes 655376 | tf_op jit(solution)/shard_map/reduce_scatter | solution.py:65
  96.0 0.0 copy-start.1
  96.0 0.0 copy-start.3
  96.0 1.6 fusion.29
  97.7 1.6 multiply_reduce_fusion
  99.3 0.0 copy-done.4
  99.3 0.0 copy-done.1
  99.3 0.0 copy-done.3
  99.3 1.1 multiply_convert_fusion
  100.5 2.3 reshape.66
  102.7 8.3 %convolution_convert_fusion.3 = bf16[128,1280]{1,0:T(8,128)(2,1)} fusion(bf16[64,5120]{1,0:T(8,128)(2,1)} %reshape.66, bf16[5120,1280]{1,0:T(8,128)(2,1)} %param.18, s32[64]{0:T(128)S(1)} %multiply_add_fusion), kind=kOutput, calls=%fused_computation.21 | convolution fusion | flops 860086272 | bytes 14090496 | tf_op jit(solution)/shard_map/dot_general | solution.py:81
  111.0 0.0 copy-start.5
  111.0 1.8 all_to_all.8
  112.8 9.2 %all-to-all-start = ((bf16[32,4,1280]{2,1,0:T(4,128)(2,1)}), bf16[32,4,1280]{2,1,0:T(4,128)(2,1)}, u32[]{:S(2)}, u32[]{:S(2)}) async-start(bf16[32,4,1280]{2,1,0:T(4,128)(2,1)} %all_to_all.8), calls=%async_computation.1 | async-start | bytes 655360 | tf_op jit(solution)/shard_map/all_to_all | solution.py:82
  122.0 0.0 all-gather.8.cloned.1.call-start
  122.1 0.1 copy.13
  122.1 0.1 sub.44
  122.3 0.1 fusion.32
  122.4 10.4 %all-to-all-done = bf16[32,4,1280]{2,1,0:T(4,128)(2,1)} async-done(((bf16[32,4,1280]{2,1,0:T(4,128)(2,1)}), bf16[32,4,1280]{2,1,0:T(4,128)(2,1)}, u32[]{:S(2)}, u32[]{:S(2)}) %all-to-all-start) | async-done | bytes 327712 | tf_op jit(solution)/shard_map/all_to_all | solution.py:82
  132.8 1.8 all_to_all.10
  134.5 1.4 fusion.52
  135.9 0.0 copy-start.2
  135.9 0.2 multiply_reduce_fusion.1
  136.2 0.6 copy-done.2
  136.8 0.0 copy-done.5
  136.8 0.9 multiply_convert_fusion.1
  137.7 0.0 all-gather.8.cloned.1.call-update
  137.7 0.2 reduce-scatter.5.cloned.1.call-start
  137.9 27.7 %all-gather.10.cloned.1.call-done = bf16[2560,1280]{1,0:T(8,128)(2,1)} async-done(((bf16[80,1280]{1,0:T(8,128)(2,1)}), bf16[2560,1280]{1,0:T(8,128)(2,1)}) %all-gather.10.cloned.1.call-update) | async-done | bytes 6553616 | tf_op jit(solution)/shard_map/all_gather | solution.py:57
  165.6 6.0 %fusion.51 = (bf16[32,40,1280]{2,1,0:T(8,128)(2,1)}, bf16[32,40,1280]{2,1,0:T(8,128)(2,1)}) fusion(bf16[32,80,1280]{2,1,0:T(8,128)(2,1)} %bitcast.14), kind=kLoop, calls=%fused_computation.100 | loop fusion | bytes 13107200 | tf_op jit(solution)/shard_map/slice | solution.py:98
  171.7 15.0 %all-gather.8.cloned.1.call-done = bf16[512,1280]{1,0:T(8,128)(2,1)} async-done(((bf16[128,1280]{1,0:T(8,128)(2,1)}), bf16[512,1280]{1,0:T(8,128)(2,1)}) %all-gather.8.cloned.1.call-update) | async-done | bytes 1310736 | tf_op jit(solution)/shard_map/all_gather | solution.py:97
  186.7 8.1 %convolution_convert_fusion.1 = bf16[512,1280]{1,0:T(8,128)(2,1)} fusion(bf16[1280,1280]{1,0:T(8,128)(2,1)} %bitcast.16, bf16[512,1280]{1,0:T(8,128)(2,1)} %all-gather.8.cloned.1.call-done, bf16[1280,1280]{1,0:T(8,128)(2,1)} %bitcast.15), kind=kOutput, calls=%fused_computation.11 | convolution fusion | flops 3361996800 | bytes 9175040 | tf_op jit(solution)/shard_map/dot_general | solution.py:104
  194.8 0.0 reduce-scatter.5.cloned.1.call-update
  194.9 22.7 %reduce-scatter.5.cloned.1.call-done = bf16[128,1280]{1,0:T(8,128)(2,1)} async-done(((bf16[512,1280]{1,0:T(8,128)(2,1)}), bf16[128,1280]{1,0:T(8,128)(2,1)}) %reduce-scatter.5.cloned.1.call-update) | async-done | bytes 327696 | tf_op jit(solution)/shard_map/reduce_scatter | solution.py:103
  217.6 1.9 add_convert_fusion
  (12 shorter events, 0.1 us)
Async XLA Ops:
  7.4 42.4 %copy-start = (bf16[1280,1280]{1,0:T(8,128)(2,1)S(1)}, bf16[1280,1280]{1,0:T(8,128)(2,1)}, u32[]{:S(2)}) copy-start(bf16[1280,1280]{1,0:T(8,128)(2,1)} %param.16) | copy-start | bytes 9830404
  7.4 42.4 %copy-start.6 = (f32[1280]{0:T(1024)S(1)}, f32[1280]{0:T(1024)}, u32[]{:S(2)}) copy-start(f32[1280]{0:T(1024)} %param.15) | copy-start | bytes 15364
  7.4 42.4 %all-gather.6.cloned.1.call-start = ((), (), s32[]{:S(2)}) async-start(), calls=%async_computation.3 | async-start | bytes 3276800 | tf_op jit(solution)/shard_map/all_gather | solution.py:61
  12.4 83.6 %reduce-scatter.3.cloned.1.call-start = ((), (), s32[]{:S(2)}) async-start(), calls=%async_computation.4 | async-start | bytes 3276800 | tf_op jit(solution)/shard_map/reduce_scatter | solution.py:65
  60.9 1.8 copy-start.8
  60.9 3.0 %copy-start.7 = (s32[64]{0:T(128)S(1)}, s32[64]{0:T(128)}, u32[]{:S(2)}) copy-start(s32[64]{0:T(128)} %param.20) | copy-start | bytes 772
  60.9 38.5 %copy-start.4 = (f32[1280]{0:T(1024)S(1)}, f32[1280]{0:T(1024)}, u32[]{:S(2)}) copy-start(f32[1280]{0:T(1024)} %param.17) | copy-start | bytes 15364
  60.9 104.7 %all-gather.10.cloned.1.call-start = ((), (), s32[]{:S(2)}) async-start(), calls=%async_computation.7 | async-start | bytes 6758400 | tf_op jit(solution)/shard_map/all_gather | solution.py:57
  96.0 3.3 %copy-start.1 = (bf16[256,1280]{1,0:T(8,128)(2,1)S(1)}, bf16[256,1280]{1,0:T(8,128)(2,1)}, u32[]{:S(2)}) copy-start(bf16[256,1280]{1,0:T(8,128)(2,1)} %param.12) | copy-start | bytes 1966084
  96.0 3.3 %copy-start.3 = (bf16[256,1280]{1,0:T(8,128)(2,1)S(1)}, bf16[256,1280]{1,0:T(8,128)(2,1)}, u32[]{:S(2)}) copy-start(bf16[256,1280]{1,0:T(8,128)(2,1)} %reduce-scatter.3.cloned.1.call-done) | copy-start | bytes 1966084
  111.0 25.8 %copy-start.5 = (f32[1280]{0:T(1024)S(1)}, f32[1280]{0:T(1024)}, u32[]{:S(2)}) copy-start(f32[1280]{0:T(1024)} %param.21) | copy-start | bytes 15364
  112.8 20.0 %all-to-all-start = ((bf16[32,4,1280]{2,1,0:T(4,128)(2,1)}), bf16[32,4,1280]{2,1,0:T(4,128)(2,1)}, u32[]{:S(2)}, u32[]{:S(2)}) async-start(bf16[32,4,1280]{2,1,0:T(4,128)(2,1)} %all_to_all.8), calls=%async_computation.1 | async-start | bytes 655360 | tf_op jit(solution)/shard_map/all_to_all | solution.py:82
  122.0 64.7 %all-gather.8.cloned.1.call-start = ((), (), s32[]{:S(2)}) async-start(), calls=%async_computation.5 | async-start | bytes 1638400 | tf_op jit(solution)/shard_map/all_gather | solution.py:97
  135.9 0.9 copy-start.2
  137.7 79.9 %reduce-scatter.5.cloned.1.call-start = ((), (), s32[]{:S(2)}) async-start(), calls=%async_computation.6 | async-start | bytes 1638400 | tf_op jit(solution)/shard_map/reduce_scatter | solution.py:103
Sparse Core Ops, SparseCore 0:
  12.6 37.1 all-gather.5
  61.0 34.9 reduce-scatter.2
  195.0 22.5 reduce-scatter.4
Sparse Core Ops, SparseCore 1:
  64.4 101.2 all-gather.9
  167.2 19.5 all-gather.7

commit v2 on v0

v2 whole, which is shorter than its diff:
```python
import functools

import jax
import jax.numpy as jnp
from jax import lax
from jax.experimental import pallas as pl
from jax.experimental.pallas import tpu as pltpu
from jax.sharding import PartitionSpec as P

MESH = pl.DeviceIdType.MESH
D = 1280
ROWS = 256
TOK = 128
QUARTER = 1280
HALF = 2 * QUARTER
BLK = 32
CAP = 4
PIECE = 80
COLS = 256
NCOL = D // COLS
PART = 128

S_VROW, S_UP, S_BIAS, S_DOWN, S_VBACK = 0, 2, 3, 4, 9
S_SLOT, S_A2A, S_TROW, S_TBACK = 19, 20, 21, 22
S_OX, S_QZ, S_QY, S_OY, S_QX, S_PAIR = 27, 30, 31, 34, 37, 40
N_SEM = 48


def normalize(values, row_gain):
    center = values - jnp.mean(values, axis=-1, keepdims=True)
    spread = jnp.mean(center * center, axis=-1, keepdims=True)
    return center * lax.rsqrt(spread + 1e-06) * row_gain


def gelu(v):
    return jax.nn.gelu(v, approximate=True)


def dot(a, b):
    return jnp.dot(a, b, preferred_element_type=jnp.float32)


def dot_t(a, b):
    return lax.dot_general(a, b, (((1,), (1,)), ((), ())), preferred_element_type=jnp.float32)


def before(mask):
    size = mask.shape[1]
    ahead = lax.broadcasted_iota(jnp.int32, (size, size), 0) < lax.broadcasted_iota(
        jnp.int32, (size, size), 1
    )
    ones = jnp.where(mask, 1.0, 0.0).astype(jnp.bfloat16)
    return dot(ones, jnp.where(ahead, 1.0, 0.0).astype(jnp.bfloat16)).astype(jnp.int32)


def step(
    patches,
    small,
    slots,
    vis_up,
    bias,
    vis_down,
    merge_proj,
    text_embed,
    text_up,
    text_down,
    out,
    rows_v,
    small_v,
    bias_v,
    x,
    hidden,
    up,
    down,
    proj,
    back_out,
    back_in,
    own,
    normed,
    joined,
    merged,
    send_rows,
    got_rows,
    got_f32,
    all_slots,
    embed_v,
    text_rows,
    text_w,
    tback_out,
    tback_in,
    send_sem,
    recv_sem,
    local_sem,
):
    seq, blk = lax.axis_index("seq"), lax.axis_index("blk")
    core, half = seq % 2, seq // 2
    px, py, pz = (blk // 2) % 4, blk // 8, (blk % 2) * 2 + half

    def place(cx, cy, cz, cc):
        cx, cy, cz = (cx + 4) % 4, (cy + 4) % 4, (cz + 4) % 4
        return ((cz % 2) * 2 + cc, (cy * 4 + cx) * 2 + cz // 2)

    twin = place(px, py, pz, 1 - core)
    partner = place(px, py, pz + 1 - 2 * core, 1 - core)
    other_hi = place(px, py, pz - 1 + 2 * half, core)
    along_x = [place(px + d, py, pz, core) for d in (1, -1, 2)]
    along_y = [place(px, py + d, pz, core) for d in (1, -1, 2)]

    def remote(src, dst, k, to):
        return pltpu.make_async_remote_copy(
            src_ref=src,
            dst_ref=dst,
            send_sem=send_sem.at[k],
            recv_sem=recv_sem.at[k],
            device_id=to,
            device_id_type=MESH,
        )

    def local(src, dst, k):
        return pltpu.make_async_copy(src, dst, local_sem.at[k])

    gate = pltpu.get_barrier_semaphore()

    def greet(i, carry):
        pl.semaphore_signal(
            gate, inc=1, device_id=(seq, (blk + i) % BLK), device_id_type=MESH
        )
        return carry

    for to in (twin, partner, other_hi):
        pl.semaphore_signal(gate, inc=1, device_id=to, device_id_type=MESH)
    lax.fori_loop(1, BLK, greet, 0)

    loads = [
        local(patches, rows_v, 0),
        local(small, small_v, 1),
        local(vis_up, up.at[pl.ds(0, QUARTER)], 2),
        local(bias, bias_v.at[0], 3),
        local(vis_down, down.at[pl.ds(0, QUARTER)], 4),
        local(slots, all_slots.at[blk], 5),
        local(text_embed, embed_v, 6),
        local(merge_proj, proj, 7),
    ]
    for copy in loads[:7]:
        copy.start()
    pl.semaphore_wait(gate, BLK + 2)

    twin_up = remote(vis_up, up.at[pl.ds(QUARTER, QUARTER)], S_UP, twin)
    twin_bias = remote(bias, bias_v.at[1], S_BIAS, twin)
    twin_up.start()
    twin_bias.start()
    loads[0].wait()
    loads[1].wait()

    row_copies = []
    for part in range(2):
        rows = pl.ds(part * PART, PART)
        v = rows_v[rows, :].astype(jnp.float32)
        x[pl.ds(ROWS + part * PART, PART), :] = normalize(v, small_v[0:1, :]).astype(jnp.bfloat16)
        copy = remote(x.at[pl.ds(ROWS + part * PART, PART)], x.at[rows], S_VROW + part, partner)
        copy.start()
        row_copies.append(copy)

    o_at = pl.ds(pl.multiple_of(PIECE * (4 * py + px), 16), PIECE)
    q_at = pl.ds(pl.multiple_of(HALF // 2 + PIECE * (4 * px + py), 16), PIECE)
    mine = pl.ds(pl.multiple_of(PIECE * half, 16), PIECE)
    theirs = pl.ds(pl.multiple_of(PIECE * (1 - half), 16), PIECE)
    q_out = lambda src: remote(src, text_w.at[core, q_at], S_QZ, other_hi)
    o_out = lambda src: [
        remote(src, text_w.at[core, o_at], S_OX + i, to) for i, to in enumerate(along_x)
    ]
    for which, source in ((0, text_up), (1, text_down)):

        @pl.when(core == which)
        def _():
            q_out(source.at[theirs]).start()
            local(source.at[mine], text_w.at[core, o_at], 8).start()
            for copy in o_out(source.at[mine]):
                copy.start()

    def tell(i, carry):
        remote(slots, all_slots.at[blk], S_SLOT, (seq, (blk + i) % BLK)).start()
        return carry

    lax.fori_loop(1, BLK, tell, 0)

    twin_down = [
        remote(
            vis_down.at[:, pl.ds(j * COLS, COLS)],
            down.at[pl.ds(QUARTER, QUARTER), pl.ds(j * COLS, COLS)],
            S_DOWN + j,
            twin,
        )
        for j in range(NCOL)
    ]
    for copy in twin_down:
        copy.start()
    loads[7].start()

    def up_block(rows, count, quarter):
        def body(j, carry):
            at = pl.multiple_of(j * COLS, COLS)
            h = dot_t(x[rows, :], up[pl.ds(quarter * QUARTER + at, COLS), :])
            h = h + bias_v[quarter, :, pl.ds(at, COLS)]
            hidden[rows, pl.ds(quarter * QUARTER + at, COLS)] = gelu(h).astype(jnp.bfloat16)
            return carry

        lax.fori_loop(0, NCOL, body, 0, unroll=True)

    own_rows = pl.ds(ROWS, ROWS)
    loads[2].wait()
    loads[3].wait()
    up_block(own_rows, ROWS, 0)

    q_copies = [
        remote(text_w.at[core, q_at], text_w.at[core, q_at], S_QY + i, to)
        for i, to in enumerate(along_y)
    ]
    q_out(text_w.at[core, q_at]).wait_recv()
    for copy in q_copies:
        copy.start()

    back_copies = []
    for part in range(2):
        rows = pl.ds(part * PART, PART)
        row_copies[part].wait_recv()
        up_block(rows, PART, 0)
        if part == 0:
            twin_up.wait_recv()
            twin_bias.wait_recv()
            loads[4].wait()
        up_block(rows, PART, 1)
        if part == 0:
            local(text_w.at[core, o_at], text_w.at[core, o_at], 8).wait()
            for copy in o_out(text_w.at[core, o_at]):
                copy.wait_recv()
            oy_at = pl.ds(pl.multiple_of(4 * PIECE * py, 16), 4 * PIECE)
            oy_copies = [
                remote(text_w.at[core, oy_at], text_w.at[core, oy_at], S_OY + i, to)
                for i, to in enumerate(along_y)
            ]
            for copy in oy_copies:
                copy.start()
        for j in range(NCOL):
            if part == 0:
                twin_down[j].wait_recv()
            cols = pl.ds(j * COLS, COLS)
            back_out[part, j] = dot(hidden[rows, :], down[:, cols]).astype(jnp.bfloat16)
            copy = remote(
                back_out.at[part, j], back_in.at[part, j], S_VBACK + part * NCOL + j, partner
            )
            copy.start()
            back_copies.append(copy)
        if part == 0:
            for copy in q_copies:
                copy.wait_recv()
            qx_at = pl.ds(pl.multiple_of(HALF // 2 + 4 * PIECE * px, 16), 4 * PIECE)
            qx_copies = [
                remote(text_w.at[core, qx_at], text_w.at[core, qx_at], S_QX + i, to)
                for i, to in enumerate(along_x)
            ]
            for copy in qx_copies:
                copy.start()

    pair_copies = []

    def pair_up(at):
        copy = remote(text_w.at[core, at], text_w.at[core, at], S_PAIR + len(pair_copies), twin)
        copy.start()
        pair_copies.append(copy)

    pair_up(oy_at)
    pair_up(qx_at)
    up_block(own_rows, ROWS, 1)
    for j in range(NCOL):
        cols = pl.ds(j * COLS, COLS)
        own[:, cols] = dot(hidden[own_rows, :], down[:, cols])

    remote(
        all_slots.at[pl.ds(0, BLK - 1)], all_slots.at[pl.ds(0, BLK - 1)], S_SLOT, twin
    ).wait()
    loads[5].wait()
    slot_rows = all_slots[:, 0, :]
    my_slots = all_slots[blk]
    target = (my_slots >> 7) % BLK
    to_target = lax.broadcasted_iota(jnp.int32, (BLK, 128), 0) == target
    to_target = to_target & (my_slots >= 0)
    rank = jnp.sum(jnp.where(to_target, before(to_target), 0), axis=0, keepdims=True)
    goes = jnp.where(my_slots >= 0, target * CAP + rank, -1)
    pick = lax.broadcasted_iota(jnp.int32, (BLK * CAP, 128), 0) == goes
    pick = jnp.where(pick, 1.0, 0.0).astype(jnp.bfloat16)[:, :64]

    for_me = ((slot_rows >> 7) % BLK == blk) & (slot_rows >= 0)
    rank_in = before(for_me)
    position = jnp.where(for_me, (slot_rows & (TOK - 1)) + 1, 0)
    lane = lax.broadcasted_iota(jnp.int32, (BLK, BLK * CAP), 1)
    source = lax.broadcasted_iota(jnp.int32, (BLK, BLK * CAP), 0)
    where = jnp.zeros((BLK, BLK * CAP), jnp.int32)
    for r in range(CAP):
        found = jnp.sum(jnp.where(rank_in == r, position, 0), axis=1, keepdims=True)
        where = where + jnp.where(lane == source * CAP + r, found, 0)
    where = jnp.sum(where, axis=0, keepdims=True) - 1
    placing = lax.broadcasted_iota(jnp.int32, (TOK, BLK * CAP), 0) == where
    placing = jnp.where(placing, 1.0, 0.0)

    for part in range(2):
        rows = pl.ds(part * PART, PART)
        for j in range(NCOL):
            back_copies[part * NCOL + j].wait_recv()
            cols = pl.ds(j * COLS, COLS)
            own[rows, cols] = (
                own[rows, cols]
                + back_in[part, j].astype(jnp.float32)
                + rows_v[rows, cols].astype(jnp.float32)
            )
        normed[rows, :] = normalize(own[rows, :], small_v[1:2, :]).astype(jnp.bfloat16)
    to_row = lax.broadcasted_iota(jnp.int32, (ROWS, ROWS), 0)
    from_row = lax.broadcasted_iota(jnp.int32, (ROWS, ROWS), 1)
    order = from_row == 4 * (to_row & 63) + (to_row >> 6)
    order = jnp.where(order, 1.0, 0.0).astype(jnp.bfloat16)
    for j in range(NCOL):
        moved = dot(order, normed[:, pl.ds(j * COLS, COLS)]).astype(jnp.bfloat16)
        for k in range(4):
            joined[:, pl.ds(k * D + j * COLS, COLS)] = moved[k * 64 : (k + 1) * 64, :]
    loads[7].wait()
    for j in range(NCOL):
        cols = pl.ds(j * COLS, COLS)
        merged[:, cols] = dot(joined[...], proj[:, cols]).astype(jnp.bfloat16)
    spread_rows = dot(pick, merged[...])
    for t in range(BLK):
        send_rows[t] = spread_rows[t * CAP : (t + 1) * CAP, :].astype(jnp.bfloat16)

    def send(i, carry):
        to = (blk + i) % BLK
        remote(send_rows.at[to], got_rows.at[blk], S_A2A, (seq, to)).start()
        return carry

    lax.fori_loop(1, BLK, send, 0)
    got_rows[blk] = send_rows[blk]

    for copies, base, coord in ((oy_copies, 0, py), (qx_copies, HALF // 2, px)):
        for i, d in enumerate((1, -1, 2)):
            copies[i].wait_recv()
            came = (coord - d + 4) % 4
            pair_up(pl.ds(pl.multiple_of(base + 4 * PIECE * came, 16), 4 * PIECE))

    remote(
        send_rows.at[pl.ds(0, BLK - 1)], got_rows.at[pl.ds(0, BLK - 1)], S_A2A, twin
    ).wait()
    for t in range(BLK):
        got_f32[pl.ds(t * CAP, CAP), :] = got_rows[t].astype(jnp.float32)
    loads[6].wait()
    placed = dot(placing.astype(jnp.bfloat16), got_f32[...].astype(jnp.bfloat16))
    filled = jnp.sum(placing, axis=1, keepdims=True) > 0.5
    text_rows[...] = jnp.where(filled, placed, embed_v[...].astype(jnp.float32))

    own_tok = pl.ds(TOK, TOK)
    x[own_tok, :] = normalize(text_rows[...], small_v[2:3, :]).astype(jnp.bfloat16)
    text_row = remote(x.at[own_tok], x.at[pl.ds(0, TOK)], S_TROW, partner)
    text_row.start()
    for copy in pair_copies:
        copy.wait_recv()

    def text_up_block(rows):
        def body(j, carry):
            at = pl.multiple_of(j * COLS, COLS)
            h = dot_t(x[rows, :], text_w[0, pl.ds(at, COLS), :])
            hidden[rows, pl.ds(at, COLS)] = gelu(h).astype(jnp.bfloat16)
            return carry

        lax.fori_loop(0, HALF // COLS, body, 0, unroll=True)

    text_up_block(own_tok)
    text_row.wait_recv()
    rows = pl.ds(0, TOK)
    text_up_block(rows)
    tback = []
    for j in range(NCOL):
        cols = pl.ds(j * COLS, COLS)
        tback_out[j] = dot(hidden[rows, :], text_w[1, :, cols]).astype(jnp.bfloat16)
        copy = remote(tback_out.at[j], tback_in.at[j], S_TBACK + j, partner)
        copy.start()
        tback.append(copy)
    for j in range(NCOL):
        cols = pl.ds(j * COLS, COLS)
        text_rows[:, cols] = text_rows[:, cols] + dot(hidden[own_tok, :], text_w[1, :, cols])
    for j in range(NCOL):
        cols = pl.ds(j * COLS, COLS)
        tback[j].wait_recv()
        out[:, cols] = (text_rows[:, cols] + tback_in[j].astype(jnp.float32)).astype(jnp.bfloat16)

    q_out(text_w.at[core, q_at]).wait_send()
    for copy in (
        o_out(text_w.at[core, o_at])
        + row_copies
        + [twin_up, twin_bias, text_row]
        + twin_down
        + back_copies
        + q_copies
        + oy_copies
        + qx_copies
        + pair_copies
        + tback
    ):
        copy.wait_send()


def per_device(
    patches,
    vis_gain,
    vis_up,
    vis_bias,
    vis_down,
    merge_gain,
    merge_proj,
    text_embed,
    slot_index,
    text_gain,
    text_up,
    text_down,
):
    small = jnp.stack([vis_gain, merge_gain, text_gain])
    slots = jnp.pad(slot_index, (0, 128 - slot_index.shape[0]), constant_values=-1)[None, :]
    any_ = pl.BlockSpec(memory_space=pl.ANY)
    bf16, f32 = jnp.bfloat16, jnp.float32
    vmem = pltpu.VMEM
    return pl.pallas_call(
        step,
        out_shape=jax.ShapeDtypeStruct(text_embed.shape, bf16),
        in_specs=[any_] * 10,
        out_specs=pl.BlockSpec(memory_space=pltpu.VMEM),
        scratch_shapes=[
            vmem((ROWS, D), bf16),
            vmem((3, D), f32),
            vmem((2, 1, QUARTER), f32),
            vmem((2 * ROWS, D), bf16),
            vmem((2 * ROWS, HALF), bf16),
            vmem((HALF, D), bf16),
            vmem((HALF, D), bf16),
            vmem((4 * D, D), bf16),
            vmem((2, NCOL, PART, COLS), bf16),
            vmem((2, NCOL, PART, COLS), bf16),
            vmem((ROWS, D), f32),
            vmem((ROWS, D), bf16),
            vmem((ROWS // 4, 4 * D), bf16),
            vmem((ROWS // 4, D), bf16),
            vmem((BLK, CAP, D), bf16),
            vmem((BLK, CAP, D), bf16),
            vmem((BLK * CAP, D), f32),
            vmem((BLK, 1, 128), jnp.int32),
            vmem((TOK, D), bf16),
            vmem((TOK, D), f32),
            vmem((2, HALF, D), bf16),
            vmem((NCOL, TOK, COLS), bf16),
            vmem((NCOL, TOK, COLS), bf16),
            pltpu.SemaphoreType.DMA((N_SEM,)),
            pltpu.SemaphoreType.DMA((N_SEM,)),
            pltpu.SemaphoreType.DMA((9,)),
        ],
        compiler_params=pltpu.CompilerParams(
            collective_id=0, has_side_effects=True, vmem_limit_bytes=60 * 2**20
        ),
        name="prefill",
    )(
        patches,
        small,
        slots,
        vis_up,
        vis_bias[None, :],
        vis_down,
        merge_proj,
        text_embed,
        text_up,
        text_down,
    )


def solution(mesh):
    placed = (
        P(("seq", "blk"), None),
        P(),
        P("seq", None),
        P("seq"),
        P("seq", None),
        P(),
        P(),
        P(("seq", "blk"), None),
        P(("seq", "blk")),
        P(),
        P("blk", None),
        P("blk", None),
    )
    return jax.shard_map(
        per_device, mesh=mesh, in_specs=placed, out_specs=P(("seq", "blk"), None), check_vma=False
    )
```

time: 509 us -> 93.9 us (0.18)
  waiting for transfers between devices: 413 us -> 0 us
  Pallas kernels: 0 us -> 86.6 us
  matrix products: 29.9 us -> 0 us
  starting transfers between devices: 18.6 us -> 0 us
  other arithmetic: 16.5 us -> 0.62 us
  between operations: 13.2 us -> 0.01 us
  local copies, waits for them, and re-layouts: 15.3 us -> 6.28 us
    reduce_scatter x2 -> x0, waiting for transfers between devices: 253 us -> none  [the longest x1 231 us: per_device(): lax.psum_scatter(jnp.dot(hidden, text_down, preferred_element_type=jnp.fl...]
    all_gather x2 -> x0, waiting for transfers between devices: 150 us -> none  [the longest x1 113 us: per_device(): gathered_tokens = lax.all_gather(text_normed, 'blk', axis=0, tiled=True)]
    pallas_call x0 -> x1, Pallas kernels: none -> 86.6 us  [per_device(): pl.pallas_call(step, out_shape=jax.ShapeDtypeStruct(text_embed.shape, bf1...]
    dot_general x3 -> x0, matrix products: 29.9 us -> none  [the longest x1 11.6 us: per_device(): jnp.dot(hidden, text_down, preferred_element_type=jnp.float32)]
    all_to_all x2 -> x0, starting transfers between devices: 18.3 us -> none  [the longest x1 9.22 us: per_device(): lax.all_to_all(send_rows, 'blk', split_axis=0, concat_axis=0, tiled=True)]
    all_to_all x2 -> x0, waiting for transfers between devices: 9.36 us -> none  [the longest x1 9.35 us: per_device(): lax.all_to_all(send_rows, 'blk', split_axis=0, concat_axis=0, tiled=True)]
    reduce_sum x7 -> x0, other arithmetic: 8.41 us -> none  [the longest x3 4.24 us: normalize(): spread = jnp.mean(center * center, axis=-1, keepdims=True)]
    convert_element_type x5 -> x0, other arithmetic: 7.22 us -> none  [the longest x1 2.2 us: per_device(): vis_normed = normalize(patches, vis_gain).astype(jnp.bfloat16)]
  transfers between devices with their start and end apart: 6 -> 0, of which waited for: 5 -> 0; matrix products, arithmetic and copies ran while one was open for 4% -> 0% of each run, Pallas kernels for 0% -> 0%
where the time goes in v2:
time: 93.9 us; the launch traced here: 93.5 us
  Pallas kernels  86.6 us (92%)
  local copies, waits for them, and re-layouts  6.28 us (7%)
    pallas_call x1, Pallas kernels, per_device(): pl.pallas_call(step, out_shape=jax.ShapeDtypeStruct(text_embed.shape, bf1...  86.6 us
    another operation x3, local copies, waits for them, and re-layouts, per_device(): small = jnp.stack([vis_gain, merge_gain, text_gain])  2.1 us

profile of v2, /device:TPU:1, one launch (start us, length us, event | category | flops | bytes accessed | tf_op | source)
XLA Modules:
  0.0 93.5 jit_solution(11285226117074262748)
XLA Ops:
  0.0 1.2 %pad_bitcast_fusion.slots = s32[1,128]{1,0:T(1,128)} fusion(s32[64]{0:T(128)} %param.20), kind=kLoop, calls=%fused_computation.1 | loop fusion | bytes 768 | tf_op jit(solution)/shard_map/broadcast_in_dim | solution.py:423
  1.2 0.7 stack.12
  1.9 1.3 %broadcast_in_dim.7.bias = f32[1,1280]{1,0:T(1,128)} reshape(f32[1280]{0:T(1024)} %param.15) | data formatting | bytes 10240 | tf_op jit(solution)/shard_map/broadcast_in_dim | solution.py:469
  3.2 0.7 stack.13
  3.9 0.7 stack.14
  4.6 0.6 pad_maximum_fusion.small
  5.2 86.6 %prefill.1 = bf16[128,1280]{1,0:T(8,128)(2,1)} custom-call(bf16[256,1280]{1,0:T(8,128)(2,1)} %patches.1, f32[3,1280]{1,0:T(4,128)} %pad_maximum_fusion.small, s32[1,128]{1,0:T(1,128)} %pad_bitcast_fusion.slots, bf16[1280,1280]{1,0:T(8,128)(2,1)} %vis_up.1, f32[1,1280]{1,0:T(1,128)} %broadcast_in_dim.7.bias, bf16[1280,1280]{1,0:T(8,128)(2,1)} %vis_down.1, ...), custom_call_target="tpu_custom_call" | custom-call | tf_op jit(solution)/shard_map/prefill/pallas_call | solution.py:427
  91.8 1.7 %copy.14 = bf16[128,1280]{1,0:T(8,128)(2,1)} copy(bf16[128,1280]{1,0:T(8,128)(2,1)} %prefill.1) | data formatting | bytes 655360

commit v3 on v2

v3 whole, which is shorter than its diff:
```python
import functools

import jax
import jax.numpy as jnp
from jax import lax
from jax.experimental import pallas as pl
from jax.experimental.pallas import tpu as pltpu
from jax.sharding import PartitionSpec as P

MESH = pl.DeviceIdType.MESH
D = 1280
ROWS = 256
TOK = 128
QUARTER = 1280
HALF = 2 * QUARTER
BLK = 32
CAP = 4
COLS = 256
NCOL = D // COLS
PART = 128
SIDES = 3

SHARD = 160

S_VROW, S_UP, S_BIAS, S_DOWN, S_VBACK = 0, 2, 3, 4, 9
S_SLOT, S_A2A, S_TROW, S_TBACK = 14, 15, 16, 19
S_Z, S_O, S_Q, S_PAIR = 34, 35, 39, 43
N_SEM = 51


def normalize(values, row_gain):
    center = values - jnp.mean(values, axis=-1, keepdims=True)
    spread = jnp.mean(center * center, axis=-1, keepdims=True)
    return center * lax.rsqrt(spread + 1e-06) * row_gain


def gelu(v):
    return jax.nn.gelu(v, approximate=True)


def dot(a, b):
    return jnp.dot(a, b, preferred_element_type=jnp.float32)


def dot_t(a, b):
    return lax.dot_general(a, b, (((1,), (1,)), ((), ())), preferred_element_type=jnp.float32)


def before(mask):
    size = mask.shape[1]
    ahead = lax.broadcasted_iota(jnp.int32, (size, size), 0) < lax.broadcasted_iota(
        jnp.int32, (size, size), 1
    )
    ones = jnp.where(mask, 1.0, 0.0).astype(jnp.bfloat16)
    return dot(ones, jnp.where(ahead, 1.0, 0.0).astype(jnp.bfloat16)).astype(jnp.int32)


def step(
    patches,
    vis_gain,
    vis_up,
    bias,
    vis_down,
    merge_gain,
    merge_proj,
    text_embed,
    slots,
    text_gain,
    text_up,
    text_down,
    out,
    rows_v,
    gain_v,
    bias_v,
    x,
    hidden,
    up,
    down,
    proj,
    back_out,
    back_in,
    own,
    normed,
    joined,
    merged,
    send_rows,
    got_rows,
    got_f32,
    all_slots,
    embed_v,
    text_rows,
    xt,
    text_w,
    passing,
    tback_out,
    tback_in,
    send_sem,
    recv_sem,
    local_sem,
):
    seq, blk = lax.axis_index("seq"), lax.axis_index("blk")
    core, half = seq % 2, seq // 2
    px, py, pz = (blk // 2) % 4, blk // 8, (blk % 2) * 2 + half

    def place(cx, cy, cz, cc):
        cx, cy, cz = (cx + 4) % 4, (cy + 4) % 4, (cz + 4) % 4
        return ((cz % 2) * 2 + cc, (cy * 4 + cx) * 2 + cz // 2)

    twin = place(px, py, pz, 1 - core)
    partner = place(px, py, pz + 1 - 2 * core, 1 - core)
    other_hi = place(px, py, pz - 1 + 2 * half, core)
    sides = [
        partner,
        place(px + 1 - 2 * core, py, pz, 1 - core),
        place(px, py + 1 - 2 * core, pz, 1 - core),
    ]
    odd = pz % 2
    users = [place(px + odd + 2 * i, py + odd + 2 * j, pz, core) for i in (0, 1) for j in (0, 1)]

    def remote(src, dst, k, to):
        return pltpu.make_async_remote_copy(
            src_ref=src,
            dst_ref=dst,
            send_sem=send_sem.at[k],
            recv_sem=recv_sem.at[k],
            device_id=to,
            device_id_type=MESH,
        )

    def local(src, dst, k):
        return pltpu.make_async_copy(src, dst, local_sem.at[k])

    gate = pltpu.get_barrier_semaphore()

    def greet(i, carry):
        pl.semaphore_signal(
            gate, inc=1, device_id=(seq, (blk + i) % BLK), device_id_type=MESH
        )
        return carry

    for to in [twin, other_hi] + sides:
        pl.semaphore_signal(gate, inc=1, device_id=to, device_id_type=MESH)
    lax.fori_loop(1, BLK, greet, 0)

    loads = [
        local(patches, rows_v, 0),
        local(vis_gain, gain_v.at[0, 0], 1),
        local(vis_up, up.at[pl.ds(0, QUARTER)], 2),
        local(bias, bias_v.at[0, 0], 3),
        local(vis_down, down.at[pl.ds(0, QUARTER)], 4),
        local(slots, all_slots.at[blk, 0], 5),
        local(text_embed, embed_v, 6),
        local(merge_proj, proj, 7),
        local(merge_gain, gain_v.at[1, 0], 9),
        local(text_gain, gain_v.at[2, 0], 10),
    ]
    for i in (0, 1, 2, 3, 5):
        loads[i].start()
    pl.semaphore_wait(gate, BLK + 4)

    twin_up = remote(vis_up, up.at[pl.ds(QUARTER, QUARTER)], S_UP, twin)
    twin_bias = remote(bias, bias_v.at[1, 0], S_BIAS, twin)
    twin_up.start()
    twin_bias.start()
    for i in (4, 6, 8, 9):
        loads[i].start()
    loads[0].wait()
    loads[1].wait()

    row_copies = []
    for part in range(2):
        rows = pl.ds(part * PART, PART)
        v = rows_v[rows, :].astype(jnp.float32)
        x[pl.ds(ROWS + part * PART, PART), :] = normalize(v, gain_v[0]).astype(jnp.bfloat16)
        copy = remote(x.at[pl.ds(ROWS + part * PART, PART)], x.at[rows], S_VROW + part, partner)
        copy.start()
        row_copies.append(copy)

    def slot(k):
        return text_w.at[core, pl.ds(SHARD * k, SHARD)]

    def o_copy(src, k):
        return remote(src, slot(k), S_O + k, users[k])

    def q_copy(k):
        return remote(passing, slot(4 + k), S_Q + k, users[k])

    z_copy = lambda src: remote(src, passing, S_Z, other_hi)
    for which, source in ((0, text_up), (1, text_down)):

        @pl.when(core == which)
        def _():
            for k in range(1, 4):
                o_copy(source, k).start()

            @pl.when(odd == 0)
            def _():
                local(source, slot(0), 8).start()

            @pl.when(odd == 1)
            def _():
                o_copy(source, 0).start()

    def tell(i, carry):
        remote(slots, all_slots.at[blk, 0], S_SLOT, (seq, (blk + i) % BLK)).start()
        return carry

    lax.fori_loop(1, BLK, tell, 0)

    twin_down = [
        remote(
            vis_down.at[:, pl.ds(j * COLS, COLS)],
            down.at[pl.ds(QUARTER, QUARTER), pl.ds(j * COLS, COLS)],
            S_DOWN + j,
            twin,
        )
        for j in range(NCOL)
    ]
    def up_block(rows, count, quarter):
        def body(j, carry):
            at = pl.multiple_of(j * COLS, COLS)
            h = dot_t(x[rows, :], up[pl.ds(quarter * QUARTER + at, COLS), :])
            h = h + bias_v[quarter, :, pl.ds(at, COLS)]
            hidden[rows, pl.ds(quarter * QUARTER + at, COLS)] = gelu(h).astype(jnp.bfloat16)
            return carry

        lax.fori_loop(0, NCOL, body, 0, unroll=True)

    own_rows, their_rows = pl.ds(ROWS, ROWS), pl.ds(0, ROWS)
    loads[2].wait()
    loads[3].wait()
    up_block(own_rows, ROWS, 0)
    for copy in twin_down:
        copy.start()
    for which, source in ((0, text_up), (1, text_down)):

        @pl.when(core == which)
        def _():
            z_copy(source).start()

    loads[4].wait()
    first, second = pl.ds(0, QUARTER), pl.ds(QUARTER, QUARTER)
    for j in range(NCOL):
        cols = pl.ds(j * COLS, COLS)
        own[:, cols] = dot(hidden[own_rows, first], down[first, cols])
    loads[7].start()
    twin_up.wait_recv()
    twin_bias.wait_recv()
    up_block(own_rows, ROWS, 1)
    for copy in row_copies:
        copy.wait_recv()
    up_block(their_rows, ROWS, 0)
    up_block(their_rows, ROWS, 1)

    z_copy(passing).wait_recv()
    for k in range(1, 4):
        q_copy(k).start()

    @pl.when(odd == 0)
    def _():
        local(passing, slot(4), 11).start()

    @pl.when(odd == 1)
    def _():
        q_copy(0).start()

    back_copies = []
    for j in range(NCOL):
        twin_down[j].wait_recv()
        cols = pl.ds(j * COLS, COLS)
        back_out[j] = dot(hidden[their_rows, :], down[:, cols]).astype(jnp.bfloat16)
        copy = remote(back_out.at[j], back_in.at[j], S_VBACK + j, partner)
        copy.start()
        back_copies.append(copy)
    for j in range(NCOL):
        cols = pl.ds(j * COLS, COLS)
        own[:, cols] = own[:, cols] + dot(hidden[own_rows, second], down[second, cols])

    remote(
        all_slots.at[pl.ds(0, BLK - 1)], all_slots.at[pl.ds(0, BLK - 1)], S_SLOT, twin
    ).wait()
    loads[5].wait()
    slot_rows = all_slots[:, 0, :]
    my_slots = all_slots[blk]
    count = my_slots.shape[1]
    target = (my_slots >> 7) % BLK
    to_target = lax.broadcasted_iota(jnp.int32, (BLK, count), 0) == target
    rank = jnp.sum(jnp.where(to_target, before(to_target), 0), axis=0, keepdims=True)
    goes = target * CAP + rank
    pick = lax.broadcasted_iota(jnp.int32, (BLK * CAP, count), 0) == goes
    pick = jnp.where(pick, 1.0, 0.0).astype(jnp.bfloat16)

    for_me = (slot_rows >> 7) % BLK == blk
    rank_in = before(for_me)
    position = jnp.where(for_me, (slot_rows & (TOK - 1)) + 1, 0)
    lane = lax.broadcasted_iota(jnp.int32, (BLK, BLK * CAP), 1)
    source = lax.broadcasted_iota(jnp.int32, (BLK, BLK * CAP), 0)
    where = jnp.zeros((BLK, BLK * CAP), jnp.int32)
    for r in range(CAP):
        found = jnp.sum(jnp.where(rank_in == r, position, 0), axis=1, keepdims=True)
        where = where + jnp.where(lane == source * CAP + r, found, 0)
    where = jnp.sum(where, axis=0, keepdims=True) - 1
    placing = lax.broadcasted_iota(jnp.int32, (TOK, BLK * CAP), 0) == where
    placing = jnp.where(placing, 1.0, 0.0)

    for j in range(NCOL):
        back_copies[j].wait_recv()
        cols = pl.ds(j * COLS, COLS)
        own[:, cols] = (
            own[:, cols] + back_in[j].astype(jnp.float32) + rows_v[:, cols].astype(jnp.float32)
        )
    loads[8].wait()
    for part in range(2):
        rows = pl.ds(part * PART, PART)
        normed[rows, :] = normalize(own[rows, :], gain_v[1]).astype(jnp.bfloat16)
    to_row = lax.broadcasted_iota(jnp.int32, (ROWS, ROWS), 0)
    from_row = lax.broadcasted_iota(jnp.int32, (ROWS, ROWS), 1)
    order = from_row == 4 * (to_row & 63) + (to_row >> 6)
    order = jnp.where(order, 1.0, 0.0).astype(jnp.bfloat16)
    for j in range(NCOL):
        moved = dot(order, normed[:, pl.ds(j * COLS, COLS)]).astype(jnp.bfloat16)
        for k in range(4):
            joined[:, pl.ds(k * D + j * COLS, COLS)] = moved[k * 64 : (k + 1) * 64, :]
    loads[7].wait()
    for j in range(NCOL):
        cols = pl.ds(j * COLS, COLS)
        merged[:, cols] = dot(joined[...], proj[:, cols]).astype(jnp.bfloat16)
    spread_rows = dot(pick, merged[...])
    for t in range(BLK):
        send_rows[t] = spread_rows[t * CAP : (t + 1) * CAP, :].astype(jnp.bfloat16)

    def send(i, carry):
        to = (blk + i) % BLK
        remote(send_rows.at[to], got_rows.at[blk], S_A2A, (seq, to)).start()
        return carry

    lax.fori_loop(1, BLK, send, 0)
    got_rows[blk] = send_rows[blk]

    for k in range(1, 4):
        o_copy(passing, k).wait_recv()
        q_copy(k).wait_recv()

    @pl.when(odd == 0)
    def _():
        local(passing, slot(0), 8).wait()
        local(passing, slot(4), 11).wait()

    @pl.when(odd == 1)
    def _():
        o_copy(passing, 0).wait_recv()
        q_copy(0).wait_recv()

    pair_copies = [remote(slot(k), slot(k), S_PAIR + k, twin) for k in range(8)]
    for copy in pair_copies:
        copy.start()

    remote(
        send_rows.at[pl.ds(0, BLK - 1)], got_rows.at[pl.ds(0, BLK - 1)], S_A2A, twin
    ).wait()
    for t in range(BLK):
        got_f32[pl.ds(t * CAP, CAP), :] = got_rows[t].astype(jnp.float32)
    loads[6].wait()
    placed = dot(placing.astype(jnp.bfloat16), got_f32[...].astype(jnp.bfloat16))
    filled = jnp.sum(placing, axis=1, keepdims=True) > 0.5
    text_rows[...] = jnp.where(filled, placed, embed_v[...].astype(jnp.float32))

    own_tok = pl.ds(SIDES * TOK, TOK)
    loads[9].wait()
    xt[own_tok, :] = normalize(text_rows[...], gain_v[2]).astype(jnp.bfloat16)
    text_row = [
        remote(xt.at[own_tok], xt.at[pl.ds(i * TOK, TOK)], S_TROW + i, to)
        for i, to in enumerate(sides)
    ]
    for copy in text_row:
        copy.start()
    for copy in pair_copies:
        copy.wait_recv()

    def text_up_block(rows):
        def body(j, carry):
            at = pl.multiple_of(j * COLS, COLS)
            h = dot_t(xt[rows, :], text_w[0, pl.ds(at, COLS), :])
            hidden[rows, pl.ds(at, COLS)] = gelu(h).astype(jnp.bfloat16)
            return carry

        lax.fori_loop(0, NCOL, body, 0, unroll=True)

    text_up_block(own_tok)
    for j in range(NCOL):
        cols = pl.ds(j * COLS, COLS)
        text_rows[:, cols] = text_rows[:, cols] + dot(hidden[own_tok, first], text_w[1, :, cols])
    for copy in text_row:
        copy.wait_recv()
    theirs = pl.ds(0, SIDES * TOK)
    text_up_block(theirs)
    tback = []
    for j in range(NCOL):
        cols = pl.ds(j * COLS, COLS)
        part = dot(hidden[theirs, first], text_w[1, :, cols]).astype(jnp.bfloat16)
        for i, to in enumerate(sides):
            tback_out[i, j] = part[i * TOK : (i + 1) * TOK, :]
            copy = remote(tback_out.at[i, j], tback_in.at[i, j], S_TBACK + i * NCOL + j, to)
            copy.start()
            tback.append(copy)
    for j in range(NCOL):
        cols = pl.ds(j * COLS, COLS)
        total = text_rows[:, cols]
        for i in range(SIDES):
            tback[j * SIDES + i].wait_recv()
            total = total + tback_in[i, j].astype(jnp.float32)
        out[:, cols] = total.astype(jnp.bfloat16)

    z_copy(passing).wait_send()
    for k in range(1, 4):
        o_copy(passing, k).wait_send()
        q_copy(k).wait_send()

    @pl.when(odd == 1)
    def _():
        o_copy(passing, 0).wait_send()
        q_copy(0).wait_send()

    for copy in (
        row_copies
        + [twin_up, twin_bias]
        + twin_down
        + back_copies
        + pair_copies
        + text_row
        + tback
    ):
        copy.wait_send()


def per_device(
    patches,
    vis_gain,
    vis_up,
    vis_bias,
    vis_down,
    merge_gain,
    merge_proj,
    text_embed,
    slot_index,
    text_gain,
    text_up,
    text_down,
):
    any_ = pl.BlockSpec(memory_space=pl.ANY)
    bf16, f32 = jnp.bfloat16, jnp.float32
    vmem = pltpu.VMEM
    return pl.pallas_call(
        step,
        out_shape=jax.ShapeDtypeStruct(text_embed.shape, bf16),
        in_specs=[any_] * 12,
        out_specs=pl.BlockSpec(memory_space=pltpu.VMEM),
        scratch_shapes=[
            vmem((ROWS, D), bf16),
            vmem((3, 1, D), f32),
            vmem((2, 1, QUARTER), f32),
            vmem((2 * ROWS, D), bf16),
            vmem((2 * ROWS, HALF), bf16),
            vmem((HALF, D), bf16),
            vmem((HALF, D), bf16),
            vmem((4 * D, D), bf16),
            vmem((NCOL, ROWS, COLS), bf16),
            vmem((NCOL, ROWS, COLS), bf16),
            vmem((ROWS, D), f32),
            vmem((ROWS, D), bf16),
            vmem((ROWS // 4, 4 * D), bf16),
            vmem((ROWS // 4, D), bf16),
            vmem((BLK, CAP, D), bf16),
            vmem((BLK, CAP, D), bf16),
            vmem((BLK * CAP, D), f32),
            vmem((BLK, 1, slot_index.shape[0]), jnp.int32),
            vmem((TOK, D), bf16),
            vmem((TOK, D), f32),
            vmem(((SIDES + 1) * TOK, D), bf16),
            vmem((2, QUARTER, D), bf16),
            vmem((SHARD, D), bf16),
            vmem((SIDES, NCOL, TOK, COLS), bf16),
            vmem((SIDES, NCOL, TOK, COLS), bf16),
            pltpu.SemaphoreType.DMA((N_SEM,)),
            pltpu.SemaphoreType.DMA((N_SEM,)),
            pltpu.SemaphoreType.DMA((12,)),
        ],
        compiler_params=pltpu.CompilerParams(
            collective_id=0, has_side_effects=True, vmem_limit_bytes=60 * 2**20
        ),
        name="prefill",
    )(
        patches,
        vis_gain,
        vis_up,
        vis_bias,
        vis_down,
        merge_gain,
        merge_proj,
        text_embed,
        slot_index,
        text_gain,
        text_up,
        text_down,
    )


def solution(mesh):
    placed = (
        P(("seq", "blk"), None),
        P(),
        P("seq", None),
        P("seq"),
        P("seq", None),
        P(),
        P(),
        P(("seq", "blk"), None),
        P(("seq", "blk")),
        P(),
        P("blk", None),
        P("blk", None),
    )
    return jax.shard_map(
        per_device, mesh=mesh, in_specs=placed, out_specs=P(("seq", "blk"), None), check_vma=False
    )
```

time: 93.9 us -> 71.7 us (0.76)
  Pallas kernels: 86.6 us -> 69.9 us
  local copies, waits for them, and re-layouts: 6.28 us -> 1.72 us
    pallas_call x1, Pallas kernels: 86.6 us -> 69.9 us  [per_device(): pl.pallas_call(step, out_shape=jax.ShapeDtypeStruct(text_embed.shape, bf1...]
    broadcast_in_dim x2 -> x0, local copies, waits for them, and re-layouts: 2.46 us -> none  [the longest x1 1.29 us: per_device(): vis_bias[None, :]]
    another operation x3 -> x0, local copies, waits for them, and re-layouts: 2.1 us -> none  [per_device(): small = jnp.stack([vis_gain, merge_gain, text_gain])]
where the time goes in v3:
time: 71.7 us; the launch traced here: 71.6 us
  Pallas kernels  69.9 us (97%)
  local copies, waits for them, and re-layouts  1.72 us (2%)
    pallas_call x1, Pallas kernels, per_device(): pl.pallas_call(step, out_shape=jax.ShapeDtypeStruct(text_embed.shape, bf1...  69.9 us
    unnamed x1, local copies, waits for them, and re-layouts  1.72 us

profile of v3, /device:TPU:1, one launch (start us, length us, event | category | flops | bytes accessed | tf_op | source)
XLA Modules:
  0.0 71.6 jit_solution(2329542925832644508)
XLA Ops:
  0.0 69.9 %prefill.1 = bf16[128,1280]{1,0:T(8,128)(2,1)} custom-call(bf16[256,1280]{1,0:T(8,128)(2,1)} %patches.1, f32[1280]{0:T(1024)} %vis_gain.1, bf16[1280,1280]{1,0:T(8,128)(2,1)} %vis_up.1, f32[1280]{0:T(1024)} %bias.1, bf16[1280,1280]{1,0:T(8,128)(2,1)} %vis_down.1, f32[1280]{0:T(1024)} %merge_gain.1, bf16[5120,1280]{1,0:T(8,128)(2,1)} %merge_proj.1, ...), custom_call_target="tpu_custom_call" | custom-call | tf_op jit(solution)/shard_map/prefill/pallas_call | solution.py:453
  69.9 1.7 %copy.14 = bf16[128,1280]{1,0:T(8,128)(2,1)} copy(bf16[128,1280]{1,0:T(8,128)(2,1)} %prefill.1) | data formatting | bytes 655360

commit v4 on v3

--- a/solution.py
+++ b/solution.py
@@ -17,15 +17,16 @@
 CAP = 4
 COLS = 256
 NCOL = D // COLS
-PART = 128
+PART = 64
+NROW = ROWS // PART
 SIDES = 3
 
 SHARD = 160
 
-S_VROW, S_UP, S_BIAS, S_DOWN, S_VBACK = 0, 2, 3, 4, 9
-S_SLOT, S_A2A, S_TROW, S_TBACK = 14, 15, 16, 19
-S_Z, S_O, S_Q, S_PAIR = 34, 35, 39, 43
-N_SEM = 51
+S_VROW, S_UP, S_BIAS, S_DOWN, S_VBACK = 0, 4, 5, 6, 11
+S_SLOT, S_A2A, S_TROW, S_TBACK = 16, 17, 18, 21
+S_Z, S_O, S_Q, S_PAIR = 36, 38, 42, 50
+N_SEM = 62
 
 
 def normalize(values, row_gain):
@@ -97,6 +98,9 @@
     send_sem,
     recv_sem,
     local_sem,
+    line_sem,
+    plane_sem,
+    twin_sem,
 ):
     seq, blk = lax.axis_index("seq"), lax.axis_index("blk")
     core, half = seq % 2, seq // 2
@@ -131,16 +135,12 @@
         return pltpu.make_async_copy(src, dst, local_sem.at[k])
 
     gate = pltpu.get_barrier_semaphore()
-
-    def greet(i, carry):
-        pl.semaphore_signal(
-            gate, inc=1, device_id=(seq, (blk + i) % BLK), device_id_type=MESH
-        )
-        return carry
-
-    for to in [twin, other_hi] + sides:
+    line_x = [place(px + d, py, pz, core) for d in (1, 2, 3)]
+    line_y = [place(px, py + d, pz, core) for d in (1, 2, 3)]
+    across = place(px, py, pz + 2, core)
+    near = [partner, twin, other_hi, across] + line_x + line_y
+    for to in near:
         pl.semaphore_signal(gate, inc=1, device_id=to, device_id_type=MESH)
-    lax.fori_loop(1, BLK, greet, 0)
 
     loads = [
         local(patches, rows_v, 0),
@@ -156,25 +156,41 @@
     ]
     for i in (0, 1, 2, 3, 5):
         loads[i].start()
-    pl.semaphore_wait(gate, BLK + 4)
+    pl.semaphore_wait(gate, len(near))
+
+    def z_copy(src, h):
+        part = pl.ds(h * SHARD // 2, SHARD // 2)
+        return remote(src.at[part], passing.at[part], S_Z + h, other_hi)
+
+    def z_start(h):
+        for which, source in ((0, text_up), (1, text_down)):
+
+            @pl.when(core == which)
+            def _():
+                z_copy(source, h).start()
 
     twin_up = remote(vis_up, up.at[pl.ds(QUARTER, QUARTER)], S_UP, twin)
     twin_bias = remote(bias, bias_v.at[1, 0], S_BIAS, twin)
     twin_up.start()
     twin_bias.start()
+    for to in line_y:
+        pl.semaphore_signal(line_sem, inc=1, device_id=to, device_id_type=MESH)
+    pl.semaphore_signal(twin_sem, inc=1, device_id=twin, device_id_type=MESH)
     for i in (4, 6, 8, 9):
         loads[i].start()
     loads[0].wait()
     loads[1].wait()
 
     row_copies = []
-    for part in range(2):
+    for part in range(NROW):
         rows = pl.ds(part * PART, PART)
         v = rows_v[rows, :].astype(jnp.float32)
         x[pl.ds(ROWS + part * PART, PART), :] = normalize(v, gain_v[0]).astype(jnp.bfloat16)
         copy = remote(x.at[pl.ds(ROWS + part * PART, PART)], x.at[rows], S_VROW + part, partner)
         copy.start()
         row_copies.append(copy)
+    pl.semaphore_wait(line_sem, len(line_y))
+    pl.semaphore_signal(plane_sem, inc=1, device_id=across, device_id_type=MESH)
 
     def slot(k):
         return text_w.at[core, pl.ds(SHARD * k, SHARD)]
@@ -182,10 +198,42 @@
     def o_copy(src, k):
         return remote(src, slot(k), S_O + k, users[k])
 
-    def q_copy(k):
-        return remote(passing, slot(4 + k), S_Q + k, users[k])
-
-    z_copy = lambda src: remote(src, passing, S_Z, other_hi)
+    def half_slot(k, h):
+        return text_w.at[core, pl.ds(SHARD * k + SHARD // 2 * h, SHARD // 2)]
+
+    def q_copy(k, h):
+        part = passing.at[pl.ds(h * SHARD // 2, SHARD // 2)]
+        return remote(part, half_slot(4 + k, h), S_Q + 2 * k + h, users[k])
+
+    def q_local(h):
+        part = passing.at[pl.ds(h * SHARD // 2, SHARD // 2)]
+        return local(part, half_slot(4, h), 11 + h)
+
+    def pass_on(h):
+        z_copy(passing, h).wait_recv()
+        for k in range(1, 4):
+            q_copy(k, h).start()
+
+        @pl.when(odd == 0)
+        def _():
+            q_local(h).start()
+
+        @pl.when(odd == 1)
+        def _():
+            q_copy(0, h).start()
+
+    def passed_on(h):
+        for k in range(1, 4):
+            q_copy(k, h).wait_recv()
+
+        @pl.when(odd == 0)
+        def _():
+            q_local(h).wait()
+
+        @pl.when(odd == 1)
+        def _():
+            q_copy(0, h).wait_recv()
+
     for which, source in ((0, text_up), (1, text_down)):
 
         @pl.when(core == which)
@@ -201,6 +249,8 @@
             def _():
                 o_copy(source, 0).start()
 
+    pl.semaphore_wait(plane_sem, 1)
+    pl.semaphore_wait(twin_sem, 1)
     def tell(i, carry):
         remote(slots, all_slots.at[blk, 0], S_SLOT, (seq, (blk + i) % BLK)).start()
         return carry
@@ -232,12 +282,6 @@
     up_block(own_rows, ROWS, 0)
     for copy in twin_down:
         copy.start()
-    for which, source in ((0, text_up), (1, text_down)):
-
-        @pl.when(core == which)
-        def _():
-            z_copy(source).start()
-
     loads[4].wait()
     first, second = pl.ds(0, QUARTER), pl.ds(QUARTER, QUARTER)
     for j in range(NCOL):
@@ -248,21 +292,12 @@
     twin_bias.wait_recv()
     up_block(own_rows, ROWS, 1)
     for copy in row_copies:
+        copy.wait_send()
+    z_start(0)
+    for copy in row_copies:
         copy.wait_recv()
     up_block(their_rows, ROWS, 0)
     up_block(their_rows, ROWS, 1)
-
-    z_copy(passing).wait_recv()
-    for k in range(1, 4):
-        q_copy(k).start()
-
-    @pl.when(odd == 0)
-    def _():
-        local(passing, slot(4), 11).start()
-
-    @pl.when(odd == 1)
-    def _():
-        q_copy(0).start()
 
     back_copies = []
     for j in range(NCOL):
@@ -272,6 +307,7 @@
         copy = remote(back_out.at[j], back_in.at[j], S_VBACK + j, partner)
         copy.start()
         back_copies.append(copy)
+    pass_on(0)
     for j in range(NCOL):
         cols = pl.ds(j * COLS, COLS)
         own[:, cols] = own[:, cols] + dot(hidden[own_rows, second], down[second, cols])
@@ -303,14 +339,30 @@
     placing = lax.broadcasted_iota(jnp.int32, (TOK, BLK * CAP), 0) == where
     placing = jnp.where(placing, 1.0, 0.0)
 
+    for k in range(1, 4):
+        o_copy(passing, k).wait_recv()
+
+    @pl.when(odd == 0)
+    def _():
+        local(passing, slot(0), 8).wait()
+
+    @pl.when(odd == 1)
+    def _():
+        o_copy(passing, 0).wait_recv()
+
+    pair_o = [remote(slot(k), slot(k), S_PAIR + k, twin) for k in range(4)]
+    for copy in pair_o:
+        copy.start()
+
     for j in range(NCOL):
         back_copies[j].wait_recv()
         cols = pl.ds(j * COLS, COLS)
         own[:, cols] = (
             own[:, cols] + back_in[j].astype(jnp.float32) + rows_v[:, cols].astype(jnp.float32)
         )
+    z_start(1)
     loads[8].wait()
-    for part in range(2):
+    for part in range(NROW):
         rows = pl.ds(part * PART, PART)
         normed[rows, :] = normalize(own[rows, :], gain_v[1]).astype(jnp.bfloat16)
     to_row = lax.broadcasted_iota(jnp.int32, (ROWS, ROWS), 0)
@@ -336,24 +388,7 @@
 
     lax.fori_loop(1, BLK, send, 0)
     got_rows[blk] = send_rows[blk]
-
-    for k in range(1, 4):
-        o_copy(passing, k).wait_recv()
-        q_copy(k).wait_recv()
-
-    @pl.when(odd == 0)
-    def _():
-        local(passing, slot(0), 8).wait()
-        local(passing, slot(4), 11).wait()
-
-    @pl.when(odd == 1)
-    def _():
-        o_copy(passing, 0).wait_recv()
-        q_copy(0).wait_recv()
-
-    pair_copies = [remote(slot(k), slot(k), S_PAIR + k, twin) for k in range(8)]
-    for copy in pair_copies:
-        copy.start()
+    pass_on(1)
 
     remote(
         send_rows.at[pl.ds(0, BLK - 1)], got_rows.at[pl.ds(0, BLK - 1)], S_A2A, twin
@@ -374,26 +409,29 @@
     ]
     for copy in text_row:
         copy.start()
-    for copy in pair_copies:
+
+    def text_up_block(part):
+        for start, size in ((0, 256), (256, 256), (512, 128)):
+            at = pl.ds(part * 4 * SHARD + start, size)
+            hidden[:, at] = gelu(dot_t(xt[...], text_w[0, at, :])).astype(jnp.bfloat16)
+
+    theirs = pl.ds(0, SIDES * TOK)
+    pair_q = []
+    for h in range(2):
+        passed_on(h)
+        for k in range(4):
+            part = half_slot(4 + k, h)
+            copy = remote(part, part, S_PAIR + 4 + 4 * h + k, twin)
+            copy.start()
+            pair_q.append(copy)
+    for copy in pair_o:
         copy.wait_recv()
-
-    def text_up_block(rows):
-        def body(j, carry):
-            at = pl.multiple_of(j * COLS, COLS)
-            h = dot_t(xt[rows, :], text_w[0, pl.ds(at, COLS), :])
-            hidden[rows, pl.ds(at, COLS)] = gelu(h).astype(jnp.bfloat16)
-            return carry
-
-        lax.fori_loop(0, NCOL, body, 0, unroll=True)
-
-    text_up_block(own_tok)
-    for j in range(NCOL):
-        cols = pl.ds(j * COLS, COLS)
-        text_rows[:, cols] = text_rows[:, cols] + dot(hidden[own_tok, first], text_w[1, :, cols])
     for copy in text_row:
         copy.wait_recv()
-    theirs = pl.ds(0, SIDES * TOK)
-    text_up_block(theirs)
+    text_up_block(0)
+    for copy in pair_q:
+        copy.wait_recv()
+    text_up_block(1)
     tback = []
     for j in range(NCOL):
         cols = pl.ds(j * COLS, COLS)
@@ -405,28 +443,34 @@
             tback.append(copy)
     for j in range(NCOL):
         cols = pl.ds(j * COLS, COLS)
+        text_rows[:, cols] = text_rows[:, cols] + dot(hidden[own_tok, first], text_w[1, :, cols])
+    for j in range(NCOL):
+        cols = pl.ds(j * COLS, COLS)
         total = text_rows[:, cols]
         for i in range(SIDES):
             tback[j * SIDES + i].wait_recv()
             total = total + tback_in[i, j].astype(jnp.float32)
         out[:, cols] = total.astype(jnp.bfloat16)
 
-    z_copy(passing).wait_send()
+    for h in range(2):
+        z_copy(passing, h).wait_send()
     for k in range(1, 4):
         o_copy(passing, k).wait_send()
-        q_copy(k).wait_send()
+        for h in range(2):
+            q_copy(k, h).wait_send()
 
     @pl.when(odd == 1)
     def _():
         o_copy(passing, 0).wait_send()
-        q_copy(0).wait_send()
+        for h in range(2):
+            q_copy(0, h).wait_send()
 
     for copy in (
-        row_copies
-        + [twin_up, twin_bias]
+        [twin_up, twin_bias]
         + twin_down
         + back_copies
-        + pair_copies
+        + pair_o
+        + pair_q
         + text_row
         + tback
     ):
@@ -483,7 +527,10 @@
             vmem((SIDES, NCOL, TOK, COLS), bf16),
             pltpu.SemaphoreType.DMA((N_SEM,)),
             pltpu.SemaphoreType.DMA((N_SEM,)),
-            pltpu.SemaphoreType.DMA((12,)),
+            pltpu.SemaphoreType.DMA((13,)),
+            pltpu.SemaphoreType.REGULAR,
+            pltpu.SemaphoreType.REGULAR,
+            pltpu.SemaphoreType.REGULAR,
         ],
         compiler_params=pltpu.CompilerParams(
             collective_id=0, has_side_effects=True, vmem_limit_bytes=60 * 2**20

time: 71.7 us -> 71.1 us (level)
  Pallas kernels: 69.9 us -> 69.1 us
    pallas_call x1, Pallas kernels: 69.9 us -> 69.1 us  [per_device(): pl.pallas_call(step, out_shape=jax.ShapeDtypeStruct(text_embed.shape, bf1...]
where the time goes in v4:
time: 71.1 us; the launch traced here: 70.8 us
  Pallas kernels  69.1 us (97%)
  local copies, waits for them, and re-layouts  1.72 us (2%)
    pallas_call x1, Pallas kernels, per_device(): pl.pallas_call(step, out_shape=jax.ShapeDtypeStruct(text_embed.shape, bf1...  69.1 us
    unnamed x1, local copies, waits for them, and re-layouts  1.72 us

profile of v4, /device:TPU:1, one launch (start us, length us, event | category | flops | bytes accessed | tf_op | source)
XLA Modules:
  0.0 70.8 jit_solution(2027699852390303326)
XLA Ops:
  0.0 69.1 %prefill.1 = bf16[128,1280]{1,0:T(8,128)(2,1)} custom-call(bf16[256,1280]{1,0:T(8,128)(2,1)} %patches.1, f32[1280]{0:T(1024)} %vis_gain.1, bf16[1280,1280]{1,0:T(8,128)(2,1)} %vis_up.1, f32[1280]{0:T(1024)} %bias.1, bf16[1280,1280]{1,0:T(8,128)(2,1)} %vis_down.1, f32[1280]{0:T(1024)} %merge_gain.1, bf16[5120,1280]{1,0:T(8,128)(2,1)} %merge_proj.1, ...), custom_call_target="tpu_custom_call" | custom-call | tf_op jit(solution)/shard_map/prefill/pallas_call | solution.py:497
  69.1 1.7 %copy.14 = bf16[128,1280]{1,0:T(8,128)(2,1)} copy(bf16[128,1280]{1,0:T(8,128)(2,1)} %prefill.1) | data formatting | bytes 655360

commit v5 on v4

--- a/solution.py
+++ b/solution.py
@@ -211,8 +211,12 @@
 
     def pass_on(h):
         z_copy(passing, h).wait_recv()
-        for k in range(1, 4):
-            q_copy(k, h).start()
+        for which, order in ((0, (1, 2, 3)), (1, (2, 1, 3))):
+
+            @pl.when(core == which)
+            def _():
+                for k in order:
+                    q_copy(k, h).start()
 
         @pl.when(odd == 0)
         def _():
@@ -238,7 +242,7 @@
 
         @pl.when(core == which)
         def _():
-            for k in range(1, 4):
+            for k in (1, 2, 3) if which == 0 else (2, 1, 3):
                 o_copy(source, k).start()
 
             @pl.when(odd == 0)

time: 71.1 us -> 71 us (level)
  no operation moved by 1% of the time
where the time goes in v5:
time: 71 us; the launch traced here: 70.8 us
  Pallas kernels  69.1 us (97%)
  local copies, waits for them, and re-layouts  1.72 us (2%)
    pallas_call x1, Pallas kernels, per_device(): pl.pallas_call(step, out_shape=jax.ShapeDtypeStruct(text_embed.shape, bf1...  69.1 us
    unnamed x1, local copies, waits for them, and re-layouts  1.72 us

profile of v5, /device:TPU:1, one launch (start us, length us, event | category | flops | bytes accessed | tf_op | source)
XLA Modules:
  0.0 70.8 jit_solution(2543397218787965232)
XLA Ops:
  0.0 69.1 %prefill.1 = bf16[128,1280]{1,0:T(8,128)(2,1)} custom-call(bf16[256,1280]{1,0:T(8,128)(2,1)} %patches.1, f32[1280]{0:T(1024)} %vis_gain.1, bf16[1280,1280]{1,0:T(8,128)(2,1)} %vis_up.1, f32[1280]{0:T(1024)} %bias.1, bf16[1280,1280]{1,0:T(8,128)(2,1)} %vis_down.1, f32[1280]{0:T(1024)} %merge_gain.1, bf16[5120,1280]{1,0:T(8,128)(2,1)} %merge_proj.1, ...), custom_call_target="tpu_custom_call" | custom-call | tf_op jit(solution)/shard_map/prefill/pallas_call | solution.py:501
  69.1 1.7 %copy.14 = bf16[128,1280]{1,0:T(8,128)(2,1)} copy(bf16[128,1280]{1,0:T(8,128)(2,1)} %prefill.1) | data formatting | bytes 655360
